TPU v7x, 512 devices: a whole 4x4x16 slice. The times are simulated.
512 devices in a mesh: layer: 16 (over y, x), dp: 32 (over z, core).
Axes of the slice: x: 4, y: 4, z: 16, core: 2. Of those that a mesh axis runs over, the one named last changes fastest.
Arguments:
- inputs: bfloat16 [4096, 1024], P('dp'), may hold values from -6 to 6
- guess_fwd: float32 [16, 4096, 1024], P('layer', 'dp'), may hold values from -9 to 9
- guess_adj: float32 [16, 4096, 1024], P('layer', 'dp'), may hold values from -6 to 6
- weights: bfloat16 [32, 1024, 1024], P('layer', 'dp'), may hold values from -0.1875 to 0.1875
- biases: float32 [32, 1024], P('layer'), may hold values from -3 to 3
- gains: float32 [16, 1024], P('layer'), may hold values from 0.6 to 1
- cotangent: bfloat16 [4096, 1024], P('dp'), may hold values from -6 to 6
Outputs:
- block_ends: float32 [16, 4096, 1024], P('layer', 'dp')
- block_adjoints: float32 [16, 4096, 1024], P('layer', 'dp')
- weight_grad: float32 [32, 1024, 1024], P('layer', 'dp')
- coarse_ends: float32 [16, 4096, 1024], P('layer', 'dp')
- coarse_adjoints: float32 [16, 4096, 1024], P('layer', 'dp')
All inputs are finite; a program needn't handle non-finite values.
Results may differ from a plain program's by a relative error of at most 0.024.
Values may be sent and summed in bfloat16 or wider, within the bound.
No kernel may reach another device: no remote copies, remote signals or barrier semaphores. Data moves between devices by JAX's collectives and lax.ppermute only.
A program may use at most 64 MiB of HBM per device.

v0:
```python
import jax
import jax.numpy as jnp
from jax import lax
from jax.sharding import PartitionSpec as P

step_size = 0.5


def from_behind(block, axis, distance):
    devices = range(lax.axis_size(axis))
    route = [(i - distance, i) for i in devices if i - distance in devices]
    return lax.ppermute(block, axis, route)


def prefix(shard, axis, combine, identity, reverse):
    size, place = (lax.axis_size(axis), lax.axis_index(axis))
    everything = jax.tree.map(lambda part: lax.all_gather(part, axis), shard)
    start = jax.tree.map(
        lambda part, zero: jnp.broadcast_to(jnp.asarray(zero, part.dtype), part.shape),
        shard,
        identity,
    )

    def hop(k, before):
        at = size - 1 - k if reverse else k
        reached = at > place if reverse else at < place
        new = combine(before, jax.tree.map(lambda part: part[at], everything))
        return jax.tree.map(lambda a, b: jnp.where(reached, a, b), new, before)

    return lax.fori_loop(0, size, hop, start)


def combine(earlier, later):
    return (earlier[0] * later[0], earlier[1] * later[0] + later[1])


def forward_block(start, weights, biases):
    state = start
    kept = []
    slopes = []
    for j in range(weights.shape[0]):
        rounded = state.astype(jnp.bfloat16)
        active = jnp.tanh(
            jnp.dot(rounded, weights[j], preferred_element_type=jnp.float32) + biases[j]
        )
        kept.append(rounded)
        slopes.append(1.0 - active * active)
        state = state + step_size * active
    return (state, kept, slopes)


def back_layer(adjoint, weight, slope):
    scaled = (adjoint * slope).astype(jnp.bfloat16)
    moved = lax.dot_general(
        scaled, weight, (((1,), (1,)), ((), ())), preferred_element_type=jnp.float32
    )
    return (adjoint + step_size * moved, scaled)


def backward_block(end, weights, slopes):
    adjoint = end
    for j in reversed(range(weights.shape[0])):
        adjoint = back_layer(adjoint, weights[j], slopes[j])[0]
    return adjoint


def grad_term(kept_rows, scaled):
    return step_size * lax.dot_general(
        kept_rows, scaled, (((0,), (0,)), ((), ())), preferred_element_type=jnp.float32
    )


def local(inputs, guess_fwd, guess_adj, weights, biases, gains, cotangent):
    full_weights = lax.all_gather(weights, "dp", axis=1, tiled=True)
    count = lax.axis_size("layer")
    index = lax.axis_index("layer")
    is_first = index == 0
    is_last = index == count - 1
    anchor = inputs.astype(jnp.float32)
    guess = guess_fwd[0]
    identity = (jnp.ones_like(gains), jnp.zeros_like(guess))
    arrived = from_behind(guess, "layer", 1)
    start = jnp.where(is_first, anchor, arrived)
    end_state = forward_block(start, full_weights, biases)[0]
    resid = end_state - guess
    factor, carried = prefix((gains, resid), "layer", combine, identity, False)
    guess = guess + (gains * carried + resid)
    start = jnp.where(is_first, anchor, from_behind(guess, "layer", 1))
    end_state, kept, slopes = forward_block(start, full_weights, biases)
    final_adj = cotangent.astype(jnp.float32)
    lam = guess_adj[0]
    arrived_adj = from_behind(lam, "layer", -1)
    end_adj = jnp.where(is_last, final_adj, arrived_adj)
    back = backward_block(end_adj, full_weights, slopes)
    resid_adj = back - lam
    factor_adj, carried_adj = prefix((gains, resid_adj), "layer", combine, identity, True)
    lam = lam + (gains * carried_adj + resid_adj)
    end_adj = jnp.where(is_last, final_adj, from_behind(lam, "layer", -1))
    adjoint = end_adj
    grads = [None] * full_weights.shape[0]
    for j in reversed(range(full_weights.shape[0])):
        adjoint, scaled = back_layer(adjoint, full_weights[j], slopes[j])
        grads[j] = lax.psum_scatter(
            grad_term(kept[j], scaled).astype(jnp.bfloat16), "dp", scatter_dimension=0, tiled=True
        ).astype(jnp.float32)
    return (end_state[None], adjoint[None], jnp.stack(grads), guess[None], lam[None])


def solution(mesh):
    return jax.shard_map(
        local,
        mesh=mesh,
        in_specs=(
            P("dp", None),
            P("layer", "dp", None),
            P("layer", "dp", None),
            P("layer", "dp", None),
            P("layer", None),
            P("layer", None),
            P("dp", None),
        ),
        out_specs=(
            P("layer", "dp", None),
            P("layer", "dp", None),
            P("layer", "dp", None),
            P("layer", "dp", None),
            P("layer", "dp", None),
        ),
        check_vma=False,
    )
```

profile of v0, /device:TPU:6, one launch (start us, length us, event | category | flops | bytes accessed | tf_op | source)
XLA Modules:
  0.0 589.4 jit_solution(7781073490397683310)
XLA Ops:
  8.0 3.4 collective-permute-start
  12.2 11.6 %collective-permute-done = f32[128,1024]{1,0:T(8,128)S(1)} collective-permute-done((f32[128,1024]{1,0:T(8,128)}, f32[128,1024]{1,0:T(8,128)S(1)}, u32[]{:S(2)}, u32[]{:S(2)}) %collective-permute-start) | collective-permute-done | bytes 524320 | tf_op jit(solution)/shard_map/ppermute | solution.py:12
  23.7 64.4 %all-gather.8.cloned.1.call-done = bf16[2,1024,1024]{2,1,0:T(8,128)(2,1)} async-done(((bf16[2,32,1024]{2,1,0:T(8,128)(2,1)}), bf16[2,1024,1024]{2,1,0:T(8,128)(2,1)}) %all-gather.8.cloned.1.call-update) | async-done | bytes 4194320 | tf_op jit(solution)/shard_map/all_gather | solution.py:74
  88.1 2.1 fusion.24
  90.3 2.9 fusion.14
  93.2 23.8 %all-gather.3 = f32[16,1,1024]{2,1,0:T(1,128)S(1)} all-gather(f32[1,1,1024]{2,1,0:T(1,128)S(1)} %bitcast.110), channel_id=2, replica_groups=mesh['layer'=16,'dp'=32] {'layer'}, dimensions={0}, use_global_device_ids=true | all-gather | bytes 69632 | tf_op jit(solution)/shard_map/all_gather | solution.py:17
  117.1 59.2 %all-gather.10.cloned.1.call-done = f32[2048,1024]{1,0:T(8,128)} async-done(((f32[128,1024]{1,0:T(8,128)}), f32[2048,1024]{1,0:T(8,128)}) %all-gather.10.cloned.1.call-update) | async-done | bytes 8388624 | tf_op jit(solution)/shard_map/all_gather | solution.py:17
  176.3 24.4 %while.30 = (s32[]{:T(128)}, f32[128,1024]{1,0:T(8,128)S(1)}, s32[]{:T(128)}, f32[16,1,1024]{2,1,0:T(1,128)S(1)}, f32[16,128,1024]{2,1,0:T(8,128)}, /*index=5*/s32[]{:T(128)}, s32[]{:T(128)}) while((s32[]{:T(128)}, f32[128,1024]{1,0:T(8,128)S(1)}, s32[]{:T(128)}, f32[16,1,1024]{2,1,0:T(1,128)S(1)}, f32[16,128,1024]{2,1,0:T(8,128)}, ...), condition=%wide.region_1.2_spmd.clone, body=%wide.region_0.1_spmd.clone.sunk | while | flops 524292 | bytes 1585265 | solution.py:30
  176.3 1.6 fusion.54
  177.9 1.5 fusion.54
  185.5 1.5 fusion.54
  193.1 1.5 fusion.54
  200.9 3.3 collective-permute-start.1
  204.2 2.5 collective-permute-start.2
  206.8 9.5 %collective-permute-done.1 = f32[128,1024]{1,0:T(8,128)S(1)} collective-permute-done((f32[128,1024]{1,0:T(8,128)S(1)}, f32[128,1024]{1,0:T(8,128)S(1)}, u32[]{:S(2)}, u32[]{:S(2)}) %collective-permute-start.1) | collective-permute-done | bytes 524320 | tf_op jit(solution)/shard_map/ppermute | solution.py:12
  216.3 2.1 multiply_add_fusion
  218.9 2.6 collective-permute-done.2
  221.6 2.1 fusion.18
  223.7 1.7 fusion.29
  225.4 86.9 %all-gather.12.cloned.1.call-done = f32[2048,1024]{1,0:T(8,128)} async-done(((f32[128,1024]{1,0:T(8,128)}), f32[2048,1024]{1,0:T(8,128)}) %all-gather.12.cloned.1.call-update) | async-done | bytes 8388624 | tf_op jit(solution)/shard_map/all_gather | solution.py:17
  312.4 24.4 %while.31 = (s32[]{:T(128)}, f32[128,1024]{1,0:T(8,128)S(1)}, s32[]{:T(128)}, f32[16,1,1024]{2,1,0:T(1,128)S(1)}, f32[16,128,1024]{2,1,0:T(8,128)}, /*index=5*/s32[]{:T(128)}, s32[]{:T(128)}, s32[]{:T(128)}, s32[]{:T(128)}) while((s32[]{:T(128)}, f32[128,1024]{1,0:T(8,128)S(1)}, s32[]{:T(128)}, f32[16,1,1024]{2,1,0:T(1,128)S(1)}, ...), condition=%wide.region_3.4_spmd.clone, body=%wide.region_2.3_spmd.clone.sunk | while | flops 524296 | bytes 1585327 | solution.py:30
  313.9 1.5 fusion.55
  318.5 1.5 fusion.55
  337.7 2.9 collective-permute-start.3
  340.6 14.7 %collective-permute-done.3 = f32[128,1024]{1,0:T(8,128)S(1)} collective-permute-done((f32[128,1024]{1,0:T(8,128)S(1)}, f32[128,1024]{1,0:T(8,128)S(1)}, u32[]{:S(2)}, u32[]{:S(2)}) %collective-permute-start.3) | collective-permute-done | bytes 524320 | tf_op jit(solution)/shard_map/ppermute | solution.py:12
  355.4 3.0 multiply_convert_fusion
  358.5 2.4 fusion.20
  360.9 2.0 multiply_convert_fusion.1
  363.8 3.2 fusion.32
  367.1 102.4 %reduce-scatter.5.cloned.1.call-done = bf16[32,1024]{1,0:T(8,128)(2,1)} async-done(((bf16[1024,1024]{1,0:T(8,128)(2,1)}), bf16[32,1024]{1,0:T(8,128)(2,1)}) %reduce-scatter.5.cloned.1.call-update) | async-done | bytes 65552 | tf_op jit(solution)/shard_map/reduce_scatter | solution.py:103
  469.4 111.9 %reduce-scatter.3.cloned.1.call-done = bf16[32,1024]{1,0:T(8,128)(2,1)} async-done(((bf16[1024,1024]{1,0:T(8,128)(2,1)}), bf16[32,1024]{1,0:T(8,128)(2,1)}) %reduce-scatter.3.cloned.1.call-update) | async-done | bytes 65552 | tf_op jit(solution)/shard_map/reduce_scatter | solution.py:103
  581.3 1.6 maximum_convert_fusion
  (98 shorter events, 43.0 us)
Async XLA Ops:
  7.2 83.1 %copy-start.3 = (f32[1,128,1024]{2,1,0:T(8,128)S(1)}, f32[1,128,1024]{2,1,0:T(8,128)}, u32[]{:S(2)}) copy-start(f32[1,128,1024]{2,1,0:T(8,128)} %param.12) | copy-start | bytes 1572868
  7.2 86.0 %copy-start.10 = (f32[1,1024]{1,0:T(1,128)S(1)}, f32[1,1024]{1,0:T(1,128)}, u32[]{:S(2)}) copy-start(f32[1,1024]{1,0:T(1,128)} %param.16) | copy-start | bytes 12292
  7.2 80.9 %all-gather.8.cloned.1.call-start = ((), (), s32[]{:S(2)}) async-start(), calls=%async_computation.2 | async-start | bytes 4325376 | tf_op jit(solution)/shard_map/all_gather | solution.py:74
  7.9 168.4 %all-gather.10.cloned.1.call-start = ((), (), s32[]{:S(2)}) async-start(), calls=%async_computation.5 | async-start | bytes 8912896 | tf_op jit(solution)/shard_map/all_gather | solution.py:17
  8.0 15.8 %collective-permute-start = (f32[128,1024]{1,0:T(8,128)}, f32[128,1024]{1,0:T(8,128)S(1)}, u32[]{:S(2)}, u32[]{:S(2)}) collective-permute-start(f32[128,1024]{1,0:T(8,128)} %bitcast.100), channel_id=1, source_target_pairs={{0,32},{32,64},{64,96},{96,128},{128,160},{160,192},{192,224},{224... | collective-permute-start | bytes 1572872 | tf_op jit(solution)/shard_map/ppermute | solution.py:12
  93.1 107.6 %copy-start.1 = (f32[128,1024]{1,0:T(8,128)S(1)}, f32[128,1024]{1,0:T(8,128)}, u32[]{:S(2)}) copy-start(f32[128,1024]{1,0:T(8,128)} %fusion.14) | copy-start | bytes 1572868
  93.2 219.2 %all-gather.12.cloned.1.call-start = ((), (), s32[]{:S(2)}) async-start(), calls=%async_computation.6 | async-start | bytes 8912896 | tf_op jit(solution)/shard_map/all_gather | solution.py:17
  176.3 27.9 %copy-start.4 = (f32[1,128,1024]{2,1,0:T(8,128)S(1)}, f32[1,128,1024]{2,1,0:T(8,128)}, u32[]{:S(2)}) copy-start(f32[1,128,1024]{2,1,0:T(8,128)} %param.13) | copy-start | bytes 1572868
  176.3 40.0 %copy-start.5 = (bf16[128,1024]{1,0:T(8,128)(2,1)S(1)}, bf16[128,1024]{1,0:T(8,128)(2,1)}, u32[]{:S(2)}) copy-start(bf16[128,1024]{1,0:T(8,128)(2,1)} %param.11) | copy-start | bytes 786436
  200.9 18.0 %copy-start.6 = (f32[128,1024]{1,0:T(8,128)}, f32[128,1024]{1,0:T(8,128)S(1)}, u32[]{:S(2)}) copy-start(f32[128,1024]{1,0:T(8,128)S(1)} %add_add_fusion.1) | copy-start | bytes 1572868
  200.9 15.4 %collective-permute-start.1 = (f32[128,1024]{1,0:T(8,128)S(1)}, f32[128,1024]{1,0:T(8,128)S(1)}, u32[]{:S(2)}, u32[]{:S(2)}) collective-permute-start(f32[128,1024]{1,0:T(8,128)S(1)} %add_add_fusion.1), channel_id=1, source_target_pairs={{0,32},{32,64},{64,96},{96,128},{128,160},{160,192},{192,224},{224... | collective-permute-start | bytes 1572872 | tf_op jit(solution)/shard_map/ppermute | solution.py:12
  204.2 17.3 %collective-permute-start.2 = (f32[128,1024]{1,0:T(8,128)S(1)}, f32[128,1024]{1,0:T(8,128)}, u32[]{:S(2)}, u32[]{:S(2)}) collective-permute-start(f32[128,1024]{1,0:T(8,128)S(1)} %bitcast.101), channel_id=1, source_target_pairs={{32,0},{64,32},{96,64},{128,96},{160,128},{192,160},{224,192},{256... | collective-permute-start | bytes 1572872 | tf_op jit(solution)/shard_map/ppermute | solution.py:12
  206.8 11.7 %copy-start = (bf16[2,1024,1024]{2,1,0:T(8,128)(2,1)S(1)}, bf16[2,1024,1024]{2,1,0:T(8,128)(2,1)}, u32[]{:S(2)}) copy-start(bf16[2,1024,1024]{2,1,0:T(8,128)(2,1)} %all-gather.8.cloned.1.call-done) | copy-start | bytes 12582916
  206.8 14.8 %copy-start.8 = (bf16[128,1024]{1,0:T(8,128)(2,1)S(1)}, bf16[128,1024]{1,0:T(8,128)(2,1)}, u32[]{:S(2)}) copy-start(bf16[128,1024]{1,0:T(8,128)(2,1)} %param.17) | copy-start | bytes 786436
  225.4 111.5 %copy-start.2 = (f32[128,1024]{1,0:T(8,128)S(1)}, f32[128,1024]{1,0:T(8,128)}, u32[]{:S(2)}) copy-start(f32[128,1024]{1,0:T(8,128)} %fusion.29) | copy-start | bytes 1572868
  225.4 244.1 %reduce-scatter.5.cloned.1.call-start = ((), (), s32[]{:S(2)}) async-start(), calls=%async_computation.4 | async-start | bytes 2162688 | tf_op jit(solution)/shard_map/reduce_scatter | solution.py:103
  336.9 0.8 copy-start.7
  337.7 20.7 %copy-start.9 = (bf16[128,1024]{1,0:T(8,128)(2,1)S(1)}, bf16[128,1024]{1,0:T(8,128)(2,1)}, u32[]{:S(2)}) copy-start(bf16[128,1024]{1,0:T(8,128)(2,1)} %param.17) | copy-start | bytes 786436
  337.7 17.6 %collective-permute-start.3 = (f32[128,1024]{1,0:T(8,128)S(1)}, f32[128,1024]{1,0:T(8,128)S(1)}, u32[]{:S(2)}, u32[]{:S(2)}) collective-permute-start(f32[128,1024]{1,0:T(8,128)S(1)} %add_add_fusion), channel_id=1, source_target_pairs={{32,0},{64,32},{96,64},{128,96},{160,128},{192,160},{224,192},{256... | collective-permute-start | bytes 1572872 | tf_op jit(solution)/shard_map/ppermute | solution.py:12
  358.4 222.9 %reduce-scatter.3.cloned.1.call-start = ((), (), s32[]{:S(2)}) async-start(), calls=%async_computation.3 | async-start | bytes 2162688 | tf_op jit(solution)/shard_map/reduce_scatter | solution.py:103
Sparse Core Ops, SparseCore 0:
  10.1 77.9 all-gather.7
  93.3 82.9 all-gather.9
  225.5 86.8 all-gather.11
  358.5 110.8 reduce-scatter.4
  472.1 109.1 reduce-scatter.2
where the time goes:
time: 592 us; the launch traced here: 589 us
  waiting for transfers between devices  464 us (78%)
  other arithmetic  50.3 us (8%)
  blocking collectives  23.8 us (4%)
  matrix products  22 us (4%)
  between operations  14.1 us (2%)
  starting transfers between devices  12.3 us (2%)
    reduce_scatter x2, waiting for transfers between devices, local(): lax.psum_scatter(grad_term(kept[j], scaled).astype(jnp.bfloat16), 'dp', s...  214 us
    all_gather x2, waiting for transfers between devices, prefix(): everything = jax.tree.map(lambda part: lax.all_gather(part, axis), shard)  146 us
    all_gather x1, waiting for transfers between devices, local(): full_weights = lax.all_gather(weights, 'dp', axis=1, tiled=True)  64.4 us
    select_n x32, other arithmetic, hop(): return jax.tree.map(lambda a, b: jnp.where(reached, a, b), new, before)  47.6 us
    ppermute x4, waiting for transfers between devices, from_behind(): return lax.ppermute(block, axis, route)  38.4 us
    all_gather x1, blocking collectives, prefix(): everything = jax.tree.map(lambda part: lax.all_gather(part, axis), shard)  23.8 us
    ppermute x4, starting transfers between devices, from_behind(): return lax.ppermute(block, axis, route)  12.1 us
  transfers between devices with their start and end apart: 9, of which 9 were waited for; matrix products, arithmetic and copies ran while one was open for 2% of the time, Pallas kernels for 0%

commit v1 on v0

v1 whole, which is shorter than its diff:
```python
import functools

import jax
import jax.numpy as jnp
from jax import lax
from jax.experimental import pallas as pl
from jax.experimental.pallas import tpu as pltpu
from jax.sharding import Mesh, PartitionSpec as P

step_size = 0.5
bf16 = jnp.bfloat16
f32 = jnp.float32


def from_behind(block, axis, distance):
    devices = range(lax.axis_size(axis))
    route = [(i - distance, i) for i in devices if i - distance in devices]
    return lax.ppermute(block, axis, route)


def scan_kernel(ends_ref, guess_ref, gains_ref, edge_ref, starts_ref, *, first, reverse):
    blocks, rows = ends_ref.shape[:2]
    carry = jnp.zeros(ends_ref.shape[1:], f32)
    order = range(blocks - 1, -1, -1) if reverse else range(blocks)
    step = -1 if reverse else 1
    starts_ref[order[0]] = edge_ref[...]
    for k in order[:-1]:
        guess = guess_ref[k, first : first + rows, :]
        resid = ends_ref[k].astype(f32) - guess
        carry = gains_ref[k : k + 1, :] * carry + resid
        starts_ref[k + step] = (guess + carry).astype(starts_ref.dtype)


def corrected(end, guess_rows, gains_all, edge_rows, reverse):
    blocks = lax.axis_size("layer")
    rows, width = end.shape
    pieces = end.reshape(blocks, rows // blocks, width)
    mine = lax.all_to_all(pieces, "layer", 0, 0)
    starts = pl.pallas_call(
        functools.partial(
            scan_kernel, first=rows // blocks if reverse else 0, reverse=reverse
        ),
        out_shape=jax.ShapeDtypeStruct(mine.shape, bf16),
        name="coarse_scan",
    )(mine, guess_rows, gains_all, edge_rows)
    return lax.all_to_all(starts, "layer", 0, 0).reshape(rows, width)


def fetch(weights_hbm, held, sems, layers):
    bands = sems.shape[1]
    size = held.shape[1] // bands
    copies = {}
    for l in layers:
        for n in range(bands):
            band = pl.ds(n * size, size)
            copies[l, n] = pltpu.make_async_copy(
                weights_hbm.at[l, band, :], held.at[l, band, :], sems.at[l, n]
            )
            copies[l, n].start()
    return copies


def forward_layer(rounded, l, held, biases_ref, copies, bands):
    size = held.shape[1] // bands
    total = biases_ref[l : l + 1, :]
    for n in range(bands):
        if (l, n) in copies:
            copies[l, n].wait()
        band = slice(n * size, (n + 1) * size)
        total = total + jnp.dot(
            rounded[:, band], held[l, band, :], preferred_element_type=f32
        )
    return jnp.tanh(total)


def back_step(scaled, weight):
    return step_size * lax.dot_general(
        scaled, weight, (((1,), (1,)), ((), ())), preferred_element_type=f32
    )


def relax_kernel(start_ref, w_ref, b_ref, end_ref, rounded_ref, held, sems):
    layers, bands = sems.shape
    copies = fetch(w_ref, held, sems, range(layers))
    state = start_ref[...]
    for l in range(layers):
        active = forward_layer(state.astype(bf16), l, held, b_ref, copies, bands)
        state = state + step_size * active
    end_ref[...] = state
    rounded_ref[...] = state.astype(bf16)


def both_ways_kernel(
    start_ref, w_ref, b_ref, adj_ref,
    end_ref, kept_ref, slopes_ref, back_ref, rounded_ref, held, sems,
):
    layers, bands = sems.shape
    copies = fetch(w_ref, held, sems, range(layers))
    state = start_ref[...].astype(f32)
    for l in range(layers):
        rounded = state.astype(bf16)
        kept_ref[l] = rounded
        active = forward_layer(rounded, l, held, b_ref, copies, bands)
        slopes_ref[l] = 1.0 - active * active
        state = state + step_size * active
    end_ref[...] = state
    adjoint = adj_ref[...]
    for l in reversed(range(layers)):
        scaled = (adjoint * slopes_ref[l]).astype(bf16)
        adjoint = adjoint + back_step(scaled, held[l])
    back_ref[...] = adjoint
    rounded_ref[...] = adjoint.astype(bf16)


def grads_kernel(
    core_ref, adj_ref, slopes_ref, kept_ref, w_ref,
    mine_ref, theirs_ref, adj_out_ref, scaled_ref, held, sems,
):
    layers, bands = sems.shape
    chips, _, rows, width = mine_ref.shape
    copies = fetch(w_ref, held, sems, range(1, layers))
    first = core_ref[0] == 0
    parts = 4
    adjoint = adj_ref[...].astype(f32)
    for l in reversed(range(layers)):
        scaled = (adjoint * slopes_ref[l]).astype(bf16)
        size = width // parts
        for m in range(parts):
            grad = step_size * lax.dot_general(
                kept_ref[l, :, m * size : (m + 1) * size],
                scaled,
                (((0,), (0,)), ((), ())),
                preferred_element_type=f32,
            )
            grad = grad.reshape(chips // parts, 2, rows, width)
            at = slice(m * chips // parts, (m + 1) * chips // parts)
            zero, one = grad[:, 0], grad[:, 1]
            mine_ref[at, l] = jnp.where(first, zero, one).astype(bf16)
            theirs_ref[at, l] = jnp.where(first, one, zero).astype(bf16)
        if l:
            for n in range(bands):
                copies[l, n].wait()
            adjoint = adjoint + back_step(scaled, held[l])
        else:
            adj_out_ref[...] = adjoint
            scaled_ref[...] = scaled


def call(kernel, name, outs, weights, ins, bands=4, smem=0):
    vmem = pl.BlockSpec(memory_space=pltpu.VMEM)
    specs = [pl.BlockSpec(memory_space=pltpu.SMEM)] * smem
    specs += [vmem] * (len(ins) - smem)
    at = [i for i, x in enumerate(ins) if x is weights][0]
    specs[at] = pl.BlockSpec(memory_space=pl.ANY)
    return pl.pallas_call(
        kernel,
        in_specs=specs,
        out_specs=[vmem] * len(outs),
        out_shape=[jax.ShapeDtypeStruct(*o) for o in outs],
        scratch_shapes=[
            pltpu.VMEM(weights.shape, weights.dtype),
            pltpu.SemaphoreType.DMA((weights.shape[0], bands)),
        ],
        name=name,
    )(*ins)


def local(inputs, guess_fwd, guess_adj, weights, biases, gains, cotangent):
    full_weights = lax.all_gather(weights, ("z", "c"), axis=1, tiled=True)
    layers, _, width = full_weights.shape
    count = lax.axis_size("layer")
    index = lax.axis_index("layer")
    rows = inputs.shape[0]
    own = rows // count
    guess = guess_fwd[0]
    lam = guess_adj[0]
    arrived = from_behind(guess, "layer", 1)
    arrived_adj = from_behind(lam, "layer", -1)
    gains_all = lax.all_to_all(
        jnp.broadcast_to(gains[None], (count, 1, width)), "layer", 0, 0
    ).reshape(count, width)
    guess_rows = lax.all_to_all(
        jnp.concatenate(
            [guess.reshape(count, own, width), lam.reshape(count, own, width)], 1
        ),
        "layer",
        0,
        0,
    )
    anchor_rows = lax.dynamic_slice_in_dim(inputs, own * index, own)
    final_rows = lax.dynamic_slice_in_dim(cotangent, own * index, own)
    guess_start = jnp.where(index == 0, inputs.astype(f32), arrived)
    guess_end = jnp.where(index == count - 1, cotangent.astype(f32), arrived_adj)
    guess_start, guess_end, gains_all, guess_rows, anchor_rows, final_rows = (
        lax.optimization_barrier(
            (guess_start, guess_end, gains_all, guess_rows, anchor_rows, final_rows)
        )
    )
    tall = (rows, width)
    relaxed, relaxed_low = call(
        relax_kernel, "relax", [(tall, f32), (tall, bf16)], full_weights,
        (guess_start, full_weights, biases),
    )
    start = corrected(relaxed_low, guess_rows, gains_all, anchor_rows, False)
    every = (layers, rows, width)
    end_state, kept, slopes, back, back_low = call(
        both_ways_kernel, "both_ways",
        [(tall, f32), (every, bf16), (every, f32), (tall, f32), (tall, bf16)],
        full_weights, (start, full_weights, biases, guess_end),
    )
    end_adj = corrected(back_low, guess_rows, gains_all, final_rows, True)
    core = lax.axis_index("c").astype(jnp.int32).reshape(1)
    chips, cores = lax.axis_size("z"), lax.axis_size("c")
    half = ((chips, layers, width // (chips * cores), width), bf16)
    mine, theirs, adjoint, scaled = call(
        grads_kernel, "grads", [half, half, (tall, f32), (tall, bf16)],
        full_weights, (core, end_adj, slopes, kept, full_weights), smem=1,
    )
    theirs = lax.ppermute(theirs, "c", [(0, 1), (1, 0)])
    total = lax.psum_scatter(mine + theirs, "z", scatter_dimension=0, tiled=True)
    adjoint = adjoint + back_step(scaled, full_weights[0])
    coarse = relaxed + gains * (start.astype(f32) - guess_start)
    coarse_adj = back + gains * (end_adj.astype(f32) - guess_end)
    return (
        end_state[None],
        adjoint[None],
        total[0].astype(f32),
        coarse[None],
        coarse_adj[None],
    )


def solution(mesh):
    layers, dp = mesh.devices.shape
    split = Mesh(mesh.devices.reshape(layers, dp // 2, 2), ("layer", "z", "c"))
    rows = ("z", "c")
    return jax.shard_map(
        local,
        mesh=split,
        in_specs=(
            P(rows, None),
            P("layer", rows, None),
            P("layer", rows, None),
            P("layer", rows, None),
            P("layer", None),
            P("layer", None),
            P(rows, None),
        ),
        out_specs=(
            P("layer", rows, None),
            P("layer", rows, None),
            P("layer", rows, None),
            P("layer", rows, None),
            P("layer", rows, None),
        ),
        check_vma=False,
    )
```

time: 592 us -> 251 us (0.42)
  waiting for transfers between devices: 464 us -> 127 us
  other arithmetic: 50.3 us -> 10.9 us
  Pallas kernels: 0 us -> 21.1 us
  matrix products: 22 us -> 3.21 us
  starting transfers between devices: 12.3 us -> 29.5 us
  blocking collectives: 23.8 us -> 39.7 us
    all_gather x3 -> x1, waiting for transfers between devices: 211 us -> 35.6 us  [local(): full_weights = lax.all_gather(weights, ('z', 'c'), axis=1, tiled=True)]
    reduce_scatter x2 -> x1, waiting for transfers between devices: 214 us -> 64 us  [local(): lax.psum_scatter(mine + theirs, 'z', scatter_dimension=0, tiled=True)]
    select_n x32 -> x2, other arithmetic: 47.6 us -> 1.69 us  [the longest x1 0.85 us: local(): guess_start = jnp.where(index == 0, inputs.astype(f32), arrived)]
    all_to_all x0 -> x3, blocking collectives: none -> 39.7 us  [the longest x2 26.8 us: corrected(): mine = lax.all_to_all(pieces, 'layer', 0, 0)]
    all_gather x1 -> x0, blocking collectives: 23.8 us -> none  [prefix(): everything = jax.tree.map(lambda part: lax.all_gather(part, axis), shard)]
    ppermute x4 -> x2, waiting for transfers between devices: 38.4 us -> 15.7 us  [from_behind(): return lax.ppermute(block, axis, route)]
    all_to_all x0 -> x3, starting transfers between devices: none -> 21.3 us  [the longest x1 9.13 us: local(): lax.all_to_all(jnp.broadcast_to(gains[None], (count, 1, width)), 'layer',...]
    pallas_call x0 -> x5, Pallas kernels: none -> 21.1 us  [the longest x3 17 us: call(): pl.pallas_call(kernel, in_specs=specs, out_specs=[vmem] * len(outs), out_...]
  transfers between devices with their start and end apart: 9 -> 8, of which waited for: 9 -> 7; matrix products, arithmetic and copies ran while one was open for 2% -> 4% of each run, Pallas kernels for 0% -> 0%
where the time goes in v1:
time: 251 us; the launch traced here: 250 us
  waiting for transfers between devices  127 us (51%)
  blocking collectives  39.7 us (16%)
  starting transfers between devices  29.5 us (12%)
  Pallas kernels  21.1 us (8%)
  between operations  14.3 us (6%)
  other arithmetic  10.9 us (4%)
  local copies, waits for them, and re-layouts  4.36 us (2%)
  matrix products  3.21 us (1%)
    reduce_scatter x1, waiting for transfers between devices, local(): lax.psum_scatter(mine + theirs, 'z', scatter_dimension=0, tiled=True)  64 us
    all_gather x1, waiting for transfers between devices, local(): full_weights = lax.all_gather(weights, ('z', 'c'), axis=1, tiled=True)  35.6 us
    all_to_all x2, blocking collectives, corrected(): mine = lax.all_to_all(pieces, 'layer', 0, 0)  26.8 us
    pallas_call x3, Pallas kernels, call(): pl.pallas_call(kernel, in_specs=specs, out_specs=[vmem] * len(outs), out_...  17 us
    ppermute x2, waiting for transfers between devices, from_behind(): return lax.ppermute(block, axis, route)  15.7 us
    all_to_all x1, blocking collectives, corrected(): return lax.all_to_all(starts, 'layer', 0, 0).reshape(rows, width)  12.8 us
    all_to_all x1, starting transfers between devices, local(): lax.all_to_all(jnp.broadcast_to(gains[None], (count, 1, width)), 'layer',...  9.13 us
    all_to_all x1, starting transfers between devices, local(): lax.all_to_all(jnp.concatenate([guess.reshape(count, own, width), lam.res...  6.37 us
  transfers between devices with their start and end apart: 8, of which 7 were waited for; matrix products, arithmetic and copies ran while one was open for 4% of the time, Pallas kernels for 0%

profile of v1, /device:TPU:6, one launch (start us, length us, event | category | flops | bytes accessed | tf_op | source)
XLA Modules:
  0.0 250.2 jit_solution(11206188861057280053)
XLA Ops:
  7.2 0.7 all-gather.2.cloned.1.call-update
  7.9 1.4 broadcast_in_dim.21
  9.3 9.1 %all-to-all-start = ((f32[16,1,1024]{2,1,0:T(1,128)}), f32[16,1,1024]{2,1,0:T(1,128)S(1)}, u32[]{:S(2)}, u32[]{:S(2)}) async-start(f32[16,1,1024]{2,1,0:T(1,128)} %broadcast_in_dim.21), calls=%async_computation | async-start | bytes 131072 | tf_op jit(solution)/shard_map/all_to_all | solution.py:179
  18.4 2.7 %collective-permute-start.1 = (f32[128,1024]{1,0:T(8,128)}, f32[128,1024]{1,0:T(8,128)S(1)}, u32[]{:S(2)}, u32[]{:S(2)}) collective-permute-start(f32[128,1024]{1,0:T(8,128)} %bitcast.39), channel_id=1, source_target_pairs={{32,0},{64,32},{96,64},{128,96},{160,128},{192,160},{224,192},{256... | collective-permute-start | bytes 1572872 | tf_op jit(solution)/shard_map/ppermute | solution.py:18
  21.2 2.4 pad_maximum_fusion
  24.2 6.4 %all-to-all-start.1 = ((f32[16,16,1024]{2,1,0:T(8,128)}), f32[16,16,1024]{2,1,0:T(8,128)S(1)}, u32[]{:S(2)}, u32[]{:S(2)}) async-start(f32[16,16,1024]{2,1,0:T(8,128)} %pad_maximum_fusion), calls=%async_computation.1 | async-start | bytes 2097152 | tf_op jit(solution)/shard_map/all_to_all | solution.py:182
  30.6 3.4 %collective-permute-start = (f32[128,1024]{1,0:T(8,128)S(1)}, f32[128,1024]{1,0:T(8,128)S(1)}, u32[]{:S(2)}, u32[]{:S(2)}) collective-permute-start(f32[128,1024]{1,0:T(8,128)S(1)} %bitcast.42), channel_id=1, source_target_pairs={{0,32},{32,64},{64,96},{96,128},{128,160},{160,192},{192,224},{224... | collective-permute-start | bytes 1572872 | tf_op jit(solution)/shard_map/ppermute | solution.py:18
  34.6 0.6 copy.14
  35.2 6.4 %collective-permute-done.1 = f32[128,1024]{1,0:T(8,128)S(1)} collective-permute-done((f32[128,1024]{1,0:T(8,128)}, f32[128,1024]{1,0:T(8,128)S(1)}, u32[]{:S(2)}, u32[]{:S(2)}) %collective-permute-start.1) | collective-permute-done | bytes 524320 | tf_op jit(solution)/shard_map/ppermute | solution.py:18
  41.6 0.8 convert_select_fusion.adj_ref
  42.4 9.3 %collective-permute-done = f32[128,1024]{1,0:T(8,128)S(1)} collective-permute-done((f32[128,1024]{1,0:T(8,128)S(1)}, f32[128,1024]{1,0:T(8,128)S(1)}, u32[]{:S(2)}, u32[]{:S(2)}) %collective-permute-start) | collective-permute-done | bytes 524320 | tf_op jit(solution)/shard_map/ppermute | solution.py:18
  51.8 0.8 convert_select_fusion.1.start_ref
  52.6 35.6 %all-gather.2.cloned.1.call-done.w_ref = bf16[2,1024,1024]{2,1,0:T(8,128)(2,1)} async-done(((bf16[2,32,1024]{2,1,0:T(8,128)(2,1)}), bf16[2,1024,1024]{2,1,0:T(8,128)(2,1)}) %all-gather.2.cloned.1.call-update) | async-done | bytes 4194320 | tf_op jit(solution)/shard_map/all_gather | solution.py:169
  88.2 4.4 %relax.1 = (f32[128,1024]{1,0:T(8,128)}, bf16[128,1024]{1,0:T(8,128)(2,1)}) custom-call(f32[128,1024]{1,0:T(8,128)} %convert_select_fusion.1.start_ref, bf16[2,1024,1024]{2,1,0:T(8,128)(2,1)} %all-gather.2.cloned.1.call-done.w_ref, f32[2,1024]{1,0:T(2,128)} %b_ref.3), custom_call_target="tpu_custom_call" | custom-call | tf_op jit(solution)/shard_map/relax/pallas_call | solution.py:155
  92.6 13.9 %all_to_all.30.ends_ref = bf16[16,8,1024]{2,1,0:T(8,128)(2,1)} all-to-all(bf16[16,8,1024]{2,1,0:T(8,128)(2,1)} %bitcast.44), channel_id=1, replica_groups=mesh['layer'=16,'z'=16,'c'=2] {'layer'}, dimensions={0} | all-to-all | bytes 524288 | tf_op jit(solution)/shard_map/all_to_all | solution.py:38
  106.6 2.1 coarse_scan.2
  108.7 12.8 %all_to_all.31 = bf16[16,8,1024]{2,1,0:T(8,128)(2,1)} all-to-all(bf16[16,8,1024]{2,1,0:T(8,128)(2,1)} %coarse_scan.2), channel_id=1, replica_groups=mesh['layer'=16,'z'=16,'c'=2] {'layer'}, dimensions={0} | all-to-all | bytes 524288 | tf_op jit(solution)/shard_map/all_to_all | solution.py:46
  121.5 5.9 %both_ways.1 = (f32[128,1024]{1,0:T(8,128)}, bf16[2,128,1024]{2,1,0:T(8,128)(2,1)}, f32[2,128,1024]{2,1,0:T(8,128)}, f32[128,1024]{1,0:T(8,128)}, bf16[128,1024]{1,0:T(8,128)(2,1)}) custom-call(bf16[128,1024]{1,0:T(8,128)(2,1)} %bitcast.35, bf16[2,1024,1024]{2,1,0:T(8,128)(2,1)} %all-gather.2.cloned.1.call-done.w_ref, f32[2,1024]{1,0:T(2,128)} %b_ref.3, ...), custom_call_target="tpu_custom_call" | custom-call | tf_op jit(solution)/shard_map/both_ways/pallas_call | solution.py:155
  127.4 12.9 %all_to_all.32.ends_ref = bf16[16,8,1024]{2,1,0:T(8,128)(2,1)} all-to-all(bf16[16,8,1024]{2,1,0:T(8,128)(2,1)} %bitcast.43), channel_id=1, replica_groups=mesh['layer'=16,'z'=16,'c'=2] {'layer'}, dimensions={0} | all-to-all | bytes 524288 | tf_op jit(solution)/shard_map/all_to_all | solution.py:38
  140.3 2.1 coarse_scan.3
  142.4 5.8 %all-to-all-start.5 = ((bf16[16,8,1024]{2,1,0:T(8,128)(2,1)}), bf16[16,8,1024]{2,1,0:T(8,128)(2,1)S(1)}, u32[]{:S(2)}, u32[]{:S(2)}) async-start(bf16[16,8,1024]{2,1,0:T(8,128)(2,1)} %coarse_scan.3), calls=%async_computation.5 | async-start | bytes 524288 | tf_op jit(solution)/shard_map/all_to_all | solution.py:46
  148.3 6.3 %all-to-all-done.5 = bf16[16,8,1024]{2,1,0:T(8,128)(2,1)S(1)} async-done(((bf16[16,8,1024]{2,1,0:T(8,128)(2,1)}), bf16[16,8,1024]{2,1,0:T(8,128)(2,1)S(1)}, u32[]{:S(2)}, u32[]{:S(2)}) %all-to-all-start.5) | async-done | bytes 262176 | tf_op jit(solution)/shard_map/all_to_all | solution.py:46
  154.6 0.7 copy-done.4
  155.3 6.7 %grads.1 = (bf16[16,2,32,1024]{3,2,1,0:T(8,128)(2,1)}, bf16[16,2,32,1024]{3,2,1,0:T(8,128)(2,1)}, f32[128,1024]{1,0:T(8,128)}, bf16[128,1024]{1,0:T(8,128)(2,1)}) custom-call(s32[1]{0:T(128)} %bitcast.8.core_ref, bf16[128,1024]{1,0:T(8,128)(2,1)} %bitcast.36, f32[2,128,1024]{2,1,0:T(8,128)} %get-tuple-element.31.slopes_ref, ...), custom_call_target="tpu_custom_call" | custom-call | tf_op jit(solution)/shard_map/grads/pallas_call | solution.py:155
  162.0 1.9 collective-permute-start.2
  163.9 4.3 %collective-permute-done.2 = bf16[16,2,32,1024]{3,2,1,0:T(8,128)(2,1)S(1)} collective-permute-done((bf16[16,2,32,1024]{3,2,1,0:T(8,128)(2,1)}, bf16[16,2,32,1024]{3,2,1,0:T(8,128)(2,1)S(1)}, u32[]{:S(2)}, u32[]{:S(2)}) %collective-permute-start.2) | collective-permute-done | bytes 2097184 | tf_op jit(solution)/shard_map/ppermute | solution.py:219
  168.2 3.9 %add.20 = bf16[16,2,32,1024]{3,2,1,0:T(8,128)(2,1)} add(bf16[16,2,32,1024]{3,2,1,0:T(8,128)(2,1)} %get-tuple-element.35, bf16[16,2,32,1024]{3,2,1,0:T(8,128)(2,1)S(1)} %collective-permute-done.2) | non-fusion elementwise | flops 1048576 | bytes 6291456 | tf_op jit(solution)/shard_map/add | solution.py:220
  172.3 0.9 copy-done.9
  173.3 3.2 %fusion.3 = f32[1,128,1024]{2,1,0:T(8,128)} fusion(f32[128,1024]{1,0:T(8,128)S(1)} %copy-done.9, bf16[128,1024]{1,0:T(8,128)(2,1)S(1)} %copy-done.12, bf16[2,1024,1024]{2,1,0:T(8,128)(2,1)} %all-gather.2.cloned.1.call-done.w_ref), kind=kOutput, calls=%fused_computation.4 | convolution fusion | flops 268697600 | bytes 3407872 | tf_op jit(solution)/shard_map/dot_general | solution.py:77
  176.5 1.2 add_bitcast_fusion
  177.8 64.0 %reduce-scatter.2.cloned.1.call-done = bf16[1,2,32,1024]{3,2,1,0:T(8,128)(2,1)} async-done(((bf16[16,2,32,1024]{3,2,1,0:T(8,128)(2,1)}), bf16[1,2,32,1024]{3,2,1,0:T(8,128)(2,1)}) %reduce-scatter.2.cloned.1.call-update) | async-done | bytes 131088 | tf_op jit(solution)/shard_map/reduce_scatter | solution.py:220
  241.8 1.6 bitcast_convert_fusion
  (32 shorter events, 1.5 us)
Async XLA Ops:
  7.2 81.1 %all-gather.2.cloned.1.call-start = ((), (), s32[]{:S(2)}) async-start(), calls=%async_computation.7 | async-start | bytes 4325376 | tf_op jit(solution)/shard_map/all_gather | solution.py:169
  9.3 14.9 %all-to-all-start = ((f32[16,1,1024]{2,1,0:T(1,128)}), f32[16,1,1024]{2,1,0:T(1,128)S(1)}, u32[]{:S(2)}, u32[]{:S(2)}) async-start(f32[16,1,1024]{2,1,0:T(1,128)} %broadcast_in_dim.21), calls=%async_computation | async-start | bytes 131072 | tf_op jit(solution)/shard_map/all_to_all | solution.py:179
  18.4 23.2 %collective-permute-start.1 = (f32[128,1024]{1,0:T(8,128)}, f32[128,1024]{1,0:T(8,128)S(1)}, u32[]{:S(2)}, u32[]{:S(2)}) collective-permute-start(f32[128,1024]{1,0:T(8,128)} %bitcast.39), channel_id=1, source_target_pairs={{32,0},{64,32},{96,64},{128,96},{160,128},{192,160},{224,192},{256... | collective-permute-start | bytes 1572872 | tf_op jit(solution)/shard_map/ppermute | solution.py:18
  21.1 9.4 %copy-start.6 = (f32[1,128,1024]{2,1,0:T(8,128)S(1)}, f32[1,128,1024]{2,1,0:T(8,128)}, u32[]{:S(2)}) copy-start(f32[1,128,1024]{2,1,0:T(8,128)} %param.8) | copy-start | bytes 1572868
  21.1 12.8 %copy-start.10 = (bf16[128,1024]{1,0:T(8,128)(2,1)S(1)}, bf16[128,1024]{1,0:T(8,128)(2,1)}, u32[]{:S(2)}) copy-start(bf16[128,1024]{1,0:T(8,128)(2,1)} %param.13) | copy-start | bytes 786436
  21.2 12.8 %copy-start.11 = (bf16[128,1024]{1,0:T(8,128)(2,1)S(1)}, bf16[128,1024]{1,0:T(8,128)(2,1)}, u32[]{:S(2)}) copy-start(bf16[128,1024]{1,0:T(8,128)(2,1)} %param.7) | copy-start | bytes 786436
  24.2 28.4 %all-to-all-start.1 = ((f32[16,16,1024]{2,1,0:T(8,128)}), f32[16,16,1024]{2,1,0:T(8,128)S(1)}, u32[]{:S(2)}, u32[]{:S(2)}) async-start(f32[16,16,1024]{2,1,0:T(8,128)} %pad_maximum_fusion), calls=%async_computation.1 | async-start | bytes 2097152 | tf_op jit(solution)/shard_map/all_to_all | solution.py:182
  30.6 21.2 %collective-permute-start = (f32[128,1024]{1,0:T(8,128)S(1)}, f32[128,1024]{1,0:T(8,128)S(1)}, u32[]{:S(2)}, u32[]{:S(2)}) collective-permute-start(f32[128,1024]{1,0:T(8,128)S(1)} %bitcast.42), channel_id=1, source_target_pairs={{0,32},{32,64},{64,96},{96,128},{128,160},{160,192},{192,224},{224... | collective-permute-start | bytes 1572872 | tf_op jit(solution)/shard_map/ppermute | solution.py:18
  52.6 40.0 %copy-start = (f32[16,16,1024]{2,1,0:T(8,128)}, f32[16,16,1024]{2,1,0:T(8,128)S(1)}, u32[]{:S(2)}) copy-start(f32[16,16,1024]{2,1,0:T(8,128)S(1)} %all-to-all-done.1.guess_ref) | copy-start | bytes 3145732
  142.4 12.2 %all-to-all-start.5 = ((bf16[16,8,1024]{2,1,0:T(8,128)(2,1)}), bf16[16,8,1024]{2,1,0:T(8,128)(2,1)S(1)}, u32[]{:S(2)}, u32[]{:S(2)}) async-start(bf16[16,8,1024]{2,1,0:T(8,128)(2,1)} %coarse_scan.3), calls=%async_computation.5 | async-start | bytes 524288 | tf_op jit(solution)/shard_map/all_to_all | solution.py:46
  148.2 93.5 %reduce-scatter.2.cloned.1.call-start = ((), (), s32[]{:S(2)}) async-start(), calls=%async_computation.8 | async-start | bytes 2228224 | tf_op jit(solution)/shard_map/reduce_scatter | solution.py:220
  154.6 0.7 copy-start.4
  162.0 6.3 %collective-permute-start.2 = (bf16[16,2,32,1024]{3,2,1,0:T(8,128)(2,1)}, bf16[16,2,32,1024]{3,2,1,0:T(8,128)(2,1)S(1)}, u32[]{:S(2)}, u32[]{:S(2)}) collective-permute-start(bf16[16,2,32,1024]{3,2,1,0:T(8,128)(2,1)} %get-tuple-element.36), channel_id=1, source_target_pairs={{0,1},{1,0},{2,3},{3,2},{4,5},{5,4},{6,7},{7,6},{8,9},{9,8},{10,11... | collective-permute-start | bytes 6291464 | tf_op jit(solution)/shard_map/ppermute | solution.py:219
  172.2 1.0 copy-start.9
  172.2 1.1 copy-start.12
  172.2 4.3 %copy-start.1 = (f32[128,1024]{1,0:T(8,128)S(1)}, f32[128,1024]{1,0:T(8,128)}, u32[]{:S(2)}) copy-start(f32[128,1024]{1,0:T(8,128)} %convert_select_fusion.adj_ref) | copy-start | bytes 1572868
  172.2 4.3 %copy-start.2 = (f32[128,1024]{1,0:T(8,128)S(1)}, f32[128,1024]{1,0:T(8,128)}, u32[]{:S(2)}) copy-start(f32[128,1024]{1,0:T(8,128)} %convert_select_fusion.1.start_ref) | copy-start | bytes 1572868
  172.2 4.3 %copy-start.3 = (bf16[16,8,1024]{2,1,0:T(8,128)(2,1)S(1)}, bf16[16,8,1024]{2,1,0:T(8,128)(2,1)}, u32[]{:S(2)}) copy-start(bf16[16,8,1024]{2,1,0:T(8,128)(2,1)} %all_to_all.31) | copy-start | bytes 786436
  172.2 4.3 %copy-start.5 = (bf16[16,8,1024]{2,1,0:T(8,128)(2,1)S(1)}, bf16[16,8,1024]{2,1,0:T(8,128)(2,1)}, u32[]{:S(2)}) copy-start(bf16[16,8,1024]{2,1,0:T(8,128)(2,1)} %copy-done.4) | copy-start | bytes 786436
  172.2 4.3 %copy-start.7 = (f32[128,1024]{1,0:T(8,128)S(1)}, f32[128,1024]{1,0:T(8,128)}, u32[]{:S(2)}) copy-start(f32[128,1024]{1,0:T(8,128)} %get-tuple-element.37) | copy-start | bytes 1572868
  172.2 4.3 %copy-start.8 = (f32[128,1024]{1,0:T(8,128)S(1)}, f32[128,1024]{1,0:T(8,128)}, u32[]{:S(2)}) copy-start(f32[128,1024]{1,0:T(8,128)} %get-tuple-element.38) | copy-start | bytes 1572868
  172.3 4.3 %copy-start.13 = (f32[1,1024]{1,0:T(1,128)S(1)}, f32[1,1024]{1,0:T(1,128)}, u32[]{:S(2)}) copy-start(f32[1,1024]{1,0:T(1,128)} %param.12) | copy-start | bytes 12292
Sparse Core Ops, SparseCore 0:
  10.1 78.0 all-gather.1
  172.3 69.4 reduce-scatter.1

commit v2 on v1

--- a/solution.py
+++ b/solution.py
@@ -10,6 +10,8 @@
 step_size = 0.5
 bf16 = jnp.bfloat16
 f32 = jnp.float32
+VMEM = pl.BlockSpec(memory_space=pltpu.VMEM)
+SMALL = pltpu.CompilerParams(vmem_limit_bytes=20 * 2**20)
 
 
 def from_behind(block, axis, distance):
@@ -40,9 +42,12 @@
         functools.partial(
             scan_kernel, first=rows // blocks if reverse else 0, reverse=reverse
         ),
-        out_shape=jax.ShapeDtypeStruct(mine.shape, bf16),
+        in_specs=[VMEM] * 4,
+        out_specs=VMEM,
+        out_shape=pltpu.VMEM(mine.shape, bf16),
+        compiler_params=SMALL,
         name="coarse_scan",
-    )(mine, guess_rows, gains_all, edge_rows)
+    )(*map(near, (mine, guess_rows, gains_all, edge_rows)))
     return lax.all_to_all(starts, "layer", 0, 0).reshape(rows, width)
 
 
@@ -54,7 +59,7 @@
         for n in range(bands):
             band = pl.ds(n * size, size)
             copies[l, n] = pltpu.make_async_copy(
-                weights_hbm.at[l, band, :], held.at[l, band, :], sems.at[l, n]
+                weights_hbm.at[band, l], held.at[l, band], sems.at[l, n]
             )
             copies[l, n].start()
     return copies
@@ -62,15 +67,20 @@
 
 def forward_layer(rounded, l, held, biases_ref, copies, bands):
     size = held.shape[1] // bands
+    width = held.shape[3]
     total = biases_ref[l : l + 1, :]
     for n in range(bands):
-        if (l, n) in copies:
-            copies[l, n].wait()
-        band = slice(n * size, (n + 1) * size)
+        copies[l, n].wait()
+        weight = held[l, n * size : (n + 1) * size].reshape(-1, width)
+        tall = weight.shape[0]
         total = total + jnp.dot(
-            rounded[:, band], held[l, band, :], preferred_element_type=f32
+            rounded[:, n * tall : (n + 1) * tall], weight, preferred_element_type=f32
         )
     return jnp.tanh(total)
+
+
+def square(weight):
+    return weight.reshape(-1, weight.shape[-1])
 
 
 def back_step(scaled, weight):
@@ -79,7 +89,7 @@
     )
 
 
-def relax_kernel(start_ref, w_ref, b_ref, end_ref, rounded_ref, held, sems):
+def relax_kernel(w_ref, start_ref, b_ref, end_ref, rounded_ref, held, sems):
     layers, bands = sems.shape
     copies = fetch(w_ref, held, sems, range(layers))
     state = start_ref[...]
@@ -91,7 +101,7 @@
 
 
 def both_ways_kernel(
-    start_ref, w_ref, b_ref, adj_ref,
+    w_ref, start_ref, b_ref, adj_ref,
     end_ref, kept_ref, slopes_ref, back_ref, rounded_ref, held, sems,
 ):
     layers, bands = sems.shape
@@ -99,7 +109,8 @@
     state = start_ref[...].astype(f32)
     for l in range(layers):
         rounded = state.astype(bf16)
-        kept_ref[l] = rounded
+        if l:
+            kept_ref[l - 1] = rounded
         active = forward_layer(rounded, l, held, b_ref, copies, bands)
         slopes_ref[l] = 1.0 - active * active
         state = state + step_size * active
@@ -107,13 +118,13 @@
     adjoint = adj_ref[...]
     for l in reversed(range(layers)):
         scaled = (adjoint * slopes_ref[l]).astype(bf16)
-        adjoint = adjoint + back_step(scaled, held[l])
+        adjoint = adjoint + back_step(scaled, square(held[l]))
     back_ref[...] = adjoint
     rounded_ref[...] = adjoint.astype(bf16)
 
 
 def grads_kernel(
-    core_ref, adj_ref, slopes_ref, kept_ref, w_ref,
+    core_ref, w_ref, adj_ref, slopes_ref, start_ref, kept_ref,
     mine_ref, theirs_ref, adj_out_ref, scaled_ref, held, sems,
 ):
     layers, bands = sems.shape
@@ -126,8 +137,10 @@
         scaled = (adjoint * slopes_ref[l]).astype(bf16)
         size = width // parts
         for m in range(parts):
+            columns = slice(m * size, (m + 1) * size)
+            kept = kept_ref[l - 1, :, columns] if l else start_ref[:, columns]
             grad = step_size * lax.dot_general(
-                kept_ref[l, :, m * size : (m + 1) * size],
+                kept,
                 scaled,
                 (((0,), (0,)), ((), ())),
                 preferred_element_type=f32,
@@ -140,34 +153,55 @@
         if l:
             for n in range(bands):
                 copies[l, n].wait()
-            adjoint = adjoint + back_step(scaled, held[l])
+            adjoint = adjoint + back_step(scaled, square(held[l]))
         else:
             adj_out_ref[...] = adjoint
             scaled_ref[...] = scaled
 
 
-def call(kernel, name, outs, weights, ins, bands=4, smem=0):
-    vmem = pl.BlockSpec(memory_space=pltpu.VMEM)
-    specs = [pl.BlockSpec(memory_space=pltpu.SMEM)] * smem
-    specs += [vmem] * (len(ins) - smem)
-    at = [i for i, x in enumerate(ins) if x is weights][0]
-    specs[at] = pl.BlockSpec(memory_space=pl.ANY)
+def add_kernel(mine_ref, theirs_ref, both_ref, sums, sems):
+    copies = []
+    parts = sems.shape[0]
+    size = sums.shape[0] // parts
+    for n in range(parts):
+        part = pl.ds(n * size, size)
+        sums[part] = mine_ref[part] + theirs_ref[part]
+        copies.append(
+            pltpu.make_async_copy(sums.at[part], both_ref.at[part], sems.at[n])
+        )
+        copies[n].start()
+    for copy in copies:
+        copy.wait()
+
+
+def near(x):
+    return pltpu.with_memory_space_constraint(x, pltpu.VMEM)
+
+
+FAR, NEAR = pltpu.HBM, pltpu.VMEM
+
+
+def call(kernel, name, outs, weights, ins, bands=4, scalars=()):
+    count, layers, rows, width = weights.shape
     return pl.pallas_call(
         kernel,
-        in_specs=specs,
-        out_specs=[vmem] * len(outs),
-        out_shape=[jax.ShapeDtypeStruct(*o) for o in outs],
+        in_specs=[pl.BlockSpec(memory_space=pltpu.SMEM)] * len(scalars)
+        + [pl.BlockSpec(memory_space=pl.ANY)]
+        + [VMEM] * len(ins),
+        out_specs=[VMEM] * len(outs),
+        out_shape=outs,
         scratch_shapes=[
-            pltpu.VMEM(weights.shape, weights.dtype),
-            pltpu.SemaphoreType.DMA((weights.shape[0], bands)),
+            pltpu.VMEM((layers, count, rows, width), weights.dtype),
+            pltpu.SemaphoreType.DMA((layers, bands)),
         ],
+        compiler_params=SMALL,
         name=name,
-    )(*ins)
+    )(*scalars, pltpu.with_memory_space_constraint(weights, pltpu.HBM), *map(near, ins))
 
 
 def local(inputs, guess_fwd, guess_adj, weights, biases, gains, cotangent):
-    full_weights = lax.all_gather(weights, ("z", "c"), axis=1, tiled=True)
-    layers, _, width = full_weights.shape
+    full_weights = lax.all_gather(weights, ("z", "c"))
+    _, layers, _, width = full_weights.shape
     count = lax.axis_size("layer")
     index = lax.axis_index("layer")
     rows = inputs.shape[0]
@@ -198,27 +232,37 @@
     )
     tall = (rows, width)
     relaxed, relaxed_low = call(
-        relax_kernel, "relax", [(tall, f32), (tall, bf16)], full_weights,
-        (guess_start, full_weights, biases),
+        relax_kernel, "relax", [FAR(tall, f32), NEAR(tall, bf16)],
+        full_weights, (guess_start, biases),
     )
     start = corrected(relaxed_low, guess_rows, gains_all, anchor_rows, False)
-    every = (layers, rows, width)
+    every, later = (layers, rows, width), (layers - 1, rows, width)
     end_state, kept, slopes, back, back_low = call(
         both_ways_kernel, "both_ways",
-        [(tall, f32), (every, bf16), (every, f32), (tall, f32), (tall, bf16)],
-        full_weights, (start, full_weights, biases, guess_end),
+        [FAR(tall, f32), NEAR(later, bf16), NEAR(every, f32), FAR(tall, f32), NEAR(tall, bf16)],
+        full_weights, (start, biases, guess_end),
     )
     end_adj = corrected(back_low, guess_rows, gains_all, final_rows, True)
     core = lax.axis_index("c").astype(jnp.int32).reshape(1)
     chips, cores = lax.axis_size("z"), lax.axis_size("c")
-    half = ((chips, layers, width // (chips * cores), width), bf16)
+    half = (chips, layers, width // (chips * cores), width)
     mine, theirs, adjoint, scaled = call(
-        grads_kernel, "grads", [half, half, (tall, f32), (tall, bf16)],
-        full_weights, (core, end_adj, slopes, kept, full_weights), smem=1,
+        grads_kernel, "grads",
+        [NEAR(half, bf16), NEAR(half, bf16), FAR(tall, f32), FAR(tall, bf16)],
+        full_weights, (end_adj, slopes, start, kept), scalars=(core,),
     )
     theirs = lax.ppermute(theirs, "c", [(0, 1), (1, 0)])
-    total = lax.psum_scatter(mine + theirs, "z", scatter_dimension=0, tiled=True)
-    adjoint = adjoint + back_step(scaled, full_weights[0])
+    both = pl.pallas_call(
+        add_kernel,
+        in_specs=[VMEM] * 2,
+        out_specs=pl.BlockSpec(memory_space=pl.ANY),
+        out_shape=jax.ShapeDtypeStruct(half, bf16),
+        scratch_shapes=[pltpu.VMEM(half, bf16), pltpu.SemaphoreType.DMA((4,))],
+        compiler_params=SMALL,
+        name="add_halves",
+    )(near(mine), near(theirs))
+    total = lax.psum_scatter(both, "z", scatter_dimension=0, tiled=True)
+    adjoint = adjoint + back_step(scaled, square(full_weights[:, 0]))
     coarse = relaxed + gains * (start.astype(f32) - guess_start)
     coarse_adj = back + gains * (end_adj.astype(f32) - guess_end)
     return (

time: 251 us -> 237 us (0.944)
  Pallas kernels: 21.1 us -> 13.7 us
  other arithmetic: 10.9 us -> 7.25 us
  blocking collectives: 39.7 us -> 37.1 us
    all_gather x1, waiting for transfers between devices: 35.6 us -> 30.3 us  [local(): full_weights = lax.all_gather(weights, ('z', 'c'))]
    all_to_all x1, waiting for transfers between devices: 0.61 us -> 5.55 us  [local(): lax.all_to_all(jnp.broadcast_to(gains[None], (count, 1, width)), 'layer',...]
    pallas_call x3 -> x4, Pallas kernels: 17 us -> 12.8 us  [the longest x3 11.3 us: call(): pl.pallas_call(kernel, in_specs=[pl.BlockSpec(memory_space=pltpu.SMEM)] *...]
    add x1 -> x0, other arithmetic: 3.93 us -> none  [local(): mine + theirs]
    pallas_call x2, Pallas kernels: 4.17 us -> 0.93 us  [corrected(): pl.pallas_call(functools.partial(scan_kernel, first=rows // blocks if rev...]
  transfers between devices with their start and end apart: 8 -> 8, of which waited for: 7 -> 6; matrix products, arithmetic and copies ran while one was open for 4% -> 5% of each run, Pallas kernels for 0% -> 0%
where the time goes in v2:
time: 237 us; the launch traced here: 236 us
  waiting for transfers between devices  129 us (54%)
  blocking collectives  37.1 us (16%)
  starting transfers between devices  27.7 us (12%)
  between operations  14.2 us (6%)
  Pallas kernels  13.7 us (6%)
  other arithmetic  7.25 us (3%)
  local copies, waits for them, and re-layouts  5.64 us (2%)
    reduce_scatter x1, waiting for transfers between devices, local(): total = lax.psum_scatter(both, 'z', scatter_dimension=0, tiled=True)  64.4 us
    all_gather x1, waiting for transfers between devices, local(): full_weights = lax.all_gather(weights, ('z', 'c'))  30.3 us
    all_to_all x2, blocking collectives, corrected(): mine = lax.all_to_all(pieces, 'layer', 0, 0)  25.5 us
    ppermute x2, waiting for transfers between devices, from_behind(): return lax.ppermute(block, axis, route)  17.7 us
    all_to_all x1, blocking collectives, corrected(): return lax.all_to_all(starts, 'layer', 0, 0).reshape(rows, width)  11.6 us
    pallas_call x3, Pallas kernels, call(): pl.pallas_call(kernel, in_specs=[pl.BlockSpec(memory_space=pltpu.SMEM)] *...  11.3 us
    all_to_all x1, starting transfers between devices, local(): lax.all_to_all(jnp.broadcast_to(gains[None], (count, 1, width)), 'layer',...  8.31 us
    all_to_all x1, waiting for transfers between devices, corrected(): return lax.all_to_all(starts, 'layer', 0, 0).reshape(rows, width)  6.3 us
  transfers between devices with their start and end apart: 8, of which 6 were waited for; matrix products, arithmetic and copies ran while one was open for 5% of the time, Pallas kernels for 0%

profile of v2, /device:TPU:6, one launch (start us, length us, event | category | flops | bytes accessed | tf_op | source)
XLA Modules:
  0.0 236.3 jit_solution(2328917036083953528)
XLA Ops:
  7.2 0.7 all-gather.3.cloned.1.call-update
  7.9 2.7 %collective-permute-start.1 = (f32[128,1024]{1,0:T(8,128)}, f32[128,1024]{1,0:T(8,128)S(1)}, u32[]{:S(2)}, u32[]{:S(2)}) collective-permute-start(f32[128,1024]{1,0:T(8,128)} %bitcast.41), channel_id=1, source_target_pairs={{32,0},{64,32},{96,64},{128,96},{160,128},{192,160},{224,192},{256... | collective-permute-start | bytes 1572872 | tf_op jit(solution)/shard_map/ppermute | solution.py:20
  10.6 1.4 broadcast_in_dim.21
  12.0 8.3 %all-to-all-start = ((f32[16,1,1024]{2,1,0:T(1,128)}), f32[16,1,1024]{2,1,0:T(1,128)S(1)}, u32[]{:S(2)}, u32[]{:S(2)}) async-start(f32[16,1,1024]{2,1,0:T(1,128)} %broadcast_in_dim.21), calls=%async_computation | async-start | bytes 131072 | tf_op jit(solution)/shard_map/all_to_all | solution.py:213
  20.3 2.4 %pad_maximum_fusion = f32[16,16,1024]{2,1,0:T(8,128)} fusion(f32[16,8,1024]{2,1,0:T(8,128)} %bitcast.42, f32[16,8,1024]{2,1,0:T(8,128)} %bitcast.43), kind=kLoop, calls=%fused_computation.3 | loop fusion | flops 262144 | bytes 2097152 | tf_op jit(solution)/shard_map/concatenate | solution.py:217
  22.7 5.5 %all-to-all-done = f32[16,1,1024]{2,1,0:T(1,128)S(1)} async-done(((f32[16,1,1024]{2,1,0:T(1,128)}), f32[16,1,1024]{2,1,0:T(1,128)S(1)}, u32[]{:S(2)}, u32[]{:S(2)}) %all-to-all-start) | async-done | bytes 65568 | tf_op jit(solution)/shard_map/all_to_all | solution.py:213
  28.2 5.5 %all-to-all-start.1 = ((f32[16,16,1024]{2,1,0:T(8,128)}), f32[16,16,1024]{2,1,0:T(8,128)S(1)}, u32[]{:S(2)}, u32[]{:S(2)}) async-start(f32[16,16,1024]{2,1,0:T(8,128)} %pad_maximum_fusion), calls=%async_computation.1 | async-start | bytes 2097152 | tf_op jit(solution)/shard_map/all_to_all | solution.py:216
  33.8 3.4 %collective-permute-start = (f32[128,1024]{1,0:T(8,128)S(1)}, f32[128,1024]{1,0:T(8,128)S(1)}, u32[]{:S(2)}, u32[]{:S(2)}) collective-permute-start(f32[128,1024]{1,0:T(8,128)S(1)} %bitcast.44), channel_id=1, source_target_pairs={{0,32},{32,64},{64,96},{96,128},{128,160},{160,192},{192,224},{224... | collective-permute-start | bytes 1572872 | tf_op jit(solution)/shard_map/ppermute | solution.py:20
  37.1 0.7 constant_dynamic-slice_fusion
  37.9 1.0 convert_select_fusion.adj_ref
  38.9 17.7 %collective-permute-done = f32[128,1024]{1,0:T(8,128)S(1)} collective-permute-done((f32[128,1024]{1,0:T(8,128)S(1)}, f32[128,1024]{1,0:T(8,128)S(1)}, u32[]{:S(2)}, u32[]{:S(2)}) %collective-permute-start) | collective-permute-done | bytes 524320 | tf_op jit(solution)/shard_map/ppermute | solution.py:20
  56.6 1.0 convert_select_fusion.1.start_ref
  57.6 30.3 %all-gather.3.cloned.1.call-done = bf16[64,32,1024]{2,1,0:T(8,128)(2,1)} async-done(((bf16[2,32,1024]{2,1,0:T(8,128)(2,1)}), bf16[64,32,1024]{2,1,0:T(8,128)(2,1)}) %all-gather.3.cloned.1.call-update) | async-done | bytes 4194320 | tf_op jit(solution)/shard_map/all_gather | solution.py:203
  87.9 3.3 %relax.1 = (f32[128,1024]{1,0:T(8,128)}, bf16[128,1024]{1,0:T(8,128)(2,1)S(1)}) custom-call(bf16[32,2,32,1024]{3,2,1,0:T(8,128)(2,1)} %bitcast.36, f32[128,1024]{1,0:T(8,128)S(1)} %convert_select_fusion.1.start_ref, f32[2,1024]{1,0:T(2,128)S(1)} %copy-done.2), custom_call_target="tpu_custom_call" | custom-call | tf_op jit(solution)/shard_map/relax/pallas_call | solution.py:186
  91.2 13.9 %all_to_all.30.ends_ref = bf16[16,8,1024]{2,1,0:T(8,128)(2,1)S(1)} all-to-all(bf16[16,8,1024]{2,1,0:T(8,128)(2,1)S(1)} %bitcast.35), channel_id=1, replica_groups=mesh['layer'=16,'z'=16,'c'=2] {'layer'}, dimensions={0} | all-to-all | bytes 524288 | tf_op jit(solution)/shard_map/all_to_all | solution.py:40
  105.2 11.6 %all_to_all.31 = bf16[16,8,1024]{2,1,0:T(8,128)(2,1)S(1)} all-to-all(bf16[16,8,1024]{2,1,0:T(8,128)(2,1)S(1)} %coarse_scan.2), channel_id=1, replica_groups=mesh['layer'=16,'z'=16,'c'=2] {'layer'}, dimensions={0} | all-to-all | bytes 524288 | tf_op jit(solution)/shard_map/all_to_all | solution.py:51
  116.8 4.7 %both_ways.1 = (f32[128,1024]{1,0:T(8,128)}, bf16[1,128,1024]{2,1,0:T(8,128)(2,1)S(1)}, f32[2,128,1024]{2,1,0:T(8,128)S(1)}, f32[128,1024]{1,0:T(8,128)}, bf16[128,1024]{1,0:T(8,128)(2,1)S(1)}) custom-call(bf16[32,2,32,1024]{3,2,1,0:T(8,128)(2,1)} %bitcast.37, bf16[128,1024]{1,0:T(8,128)(2,1)S(1)} %bitcast.29, f32[2,1024]{1,0:T(2,128)S(1)} %copy-done.2, ...), custom_call_target="tpu_custom_call" | custom-call | tf_op jit(solution)/shard_map/both_ways/pallas_call | solution.py:186
  121.5 0.7 copy-done
  122.2 11.6 %all_to_all.32.ends_ref = bf16[16,8,1024]{2,1,0:T(8,128)(2,1)S(1)} all-to-all(bf16[16,8,1024]{2,1,0:T(8,128)(2,1)S(1)} %bitcast.34), channel_id=1, replica_groups=mesh['layer'=16,'z'=16,'c'=2] {'layer'}, dimensions={0} | all-to-all | bytes 524288 | tf_op jit(solution)/shard_map/all_to_all | solution.py:40
  133.8 0.8 coarse_scan.3
  134.6 5.8 %all-to-all-start.5 = ((bf16[16,8,1024]{2,1,0:T(8,128)(2,1)}), bf16[16,8,1024]{2,1,0:T(8,128)(2,1)S(1)}, u32[]{:S(2)}, u32[]{:S(2)}) async-start(bf16[16,8,1024]{2,1,0:T(8,128)(2,1)} %coarse_scan.3), calls=%async_computation.5 | async-start | bytes 524288 | tf_op jit(solution)/shard_map/all_to_all | solution.py:51
  140.5 6.3 %all-to-all-done.5 = bf16[16,8,1024]{2,1,0:T(8,128)(2,1)S(1)} async-done(((bf16[16,8,1024]{2,1,0:T(8,128)(2,1)}), bf16[16,8,1024]{2,1,0:T(8,128)(2,1)S(1)}, u32[]{:S(2)}, u32[]{:S(2)}) %all-to-all-start.5) | async-done | bytes 262176 | tf_op jit(solution)/shard_map/all_to_all | solution.py:51
  146.8 0.9 copy-done.1
  147.7 3.4 %grads.1 = (bf16[16,2,32,1024]{3,2,1,0:T(8,128)(2,1)S(1)}, bf16[16,2,32,1024]{3,2,1,0:T(8,128)(2,1)S(1)}, f32[128,1024]{1,0:T(8,128)}, bf16[128,1024]{1,0:T(8,128)(2,1)}) custom-call(s32[1]{0:T(128)} %bitcast.9.core_ref, bf16[32,2,32,1024]{3,2,1,0:T(8,128)(2,1)} %bitcast.38, bf16[128,1024]{1,0:T(8,128)(2,1)S(1)} %bitcast.31, ...), custom_call_target="tpu_custom_call" | custom-call | tf_op jit(solution)/shard_map/grads/pallas_call | solution.py:186
  151.1 1.9 collective-permute-start.2
  153.1 4.1 %collective-permute-done.2.theirs_ref = bf16[16,2,32,1024]{3,2,1,0:T(8,128)(2,1)S(1)} collective-permute-done((bf16[16,2,32,1024]{3,2,1,0:T(8,128)(2,1)S(1)}, bf16[16,2,32,1024]{3,2,1,0:T(8,128)(2,1)S(1)}, u32[]{:S(2)}, u32[]{:S(2)}) %collective-permute-start.2) | collective-permute-done | bytes 2097184 | tf_op jit(solution)/shard_map/ppermute | solution.py:254
  157.2 1.4 add_halves.1
  158.7 1.8 slice.4
  160.6 1.6 fusion.1
  162.2 1.2 add_bitcast_fusion
  163.5 64.4 %reduce-scatter.2.cloned.1.call-done = bf16[1,2,32,1024]{3,2,1,0:T(8,128)(2,1)} async-done(((bf16[16,2,32,1024]{3,2,1,0:T(8,128)(2,1)}), bf16[1,2,32,1024]{3,2,1,0:T(8,128)(2,1)}) %reduce-scatter.2.cloned.1.call-update) | async-done | bytes 131088 | tf_op jit(solution)/shard_map/reduce_scatter | solution.py:264
  227.8 1.6 bitcast_convert_fusion
  (23 shorter events, 0.3 us)
Async XLA Ops:
  7.2 80.8 %all-gather.3.cloned.1.call-start = ((), (), s32[]{:S(2)}) async-start(), calls=%async_computation.8 | async-start | bytes 4325376 | tf_op jit(solution)/shard_map/all_gather | solution.py:203
  7.9 30.0 %collective-permute-start.1 = (f32[128,1024]{1,0:T(8,128)}, f32[128,1024]{1,0:T(8,128)S(1)}, u32[]{:S(2)}, u32[]{:S(2)}) collective-permute-start(f32[128,1024]{1,0:T(8,128)} %bitcast.41), channel_id=1, source_target_pairs={{32,0},{64,32},{96,64},{128,96},{160,128},{192,160},{224,192},{256... | collective-permute-start | bytes 1572872 | tf_op jit(solution)/shard_map/ppermute | solution.py:20
  12.0 16.2 %all-to-all-start = ((f32[16,1,1024]{2,1,0:T(1,128)}), f32[16,1,1024]{2,1,0:T(1,128)S(1)}, u32[]{:S(2)}, u32[]{:S(2)}) async-start(f32[16,1,1024]{2,1,0:T(1,128)} %broadcast_in_dim.21), calls=%async_computation | async-start | bytes 131072 | tf_op jit(solution)/shard_map/all_to_all | solution.py:213
  20.3 13.4 %copy-start.3 = (f32[1,128,1024]{2,1,0:T(8,128)S(1)}, f32[1,128,1024]{2,1,0:T(8,128)}, u32[]{:S(2)}) copy-start(f32[1,128,1024]{2,1,0:T(8,128)} %param.8) | copy-start | bytes 1572868
  22.7 65.2 %copy-start.2 = (f32[2,1024]{1,0:T(2,128)S(1)}, f32[2,1024]{1,0:T(2,128)}, u32[]{:S(2)}) copy-start(f32[2,1024]{1,0:T(2,128)} %b_ref.3) | copy-start | bytes 24580
  28.2 29.4 %all-to-all-start.1 = ((f32[16,16,1024]{2,1,0:T(8,128)}), f32[16,16,1024]{2,1,0:T(8,128)S(1)}, u32[]{:S(2)}, u32[]{:S(2)}) async-start(f32[16,16,1024]{2,1,0:T(8,128)} %pad_maximum_fusion), calls=%async_computation.1 | async-start | bytes 2097152 | tf_op jit(solution)/shard_map/all_to_all | solution.py:216
  33.8 22.8 %collective-permute-start = (f32[128,1024]{1,0:T(8,128)S(1)}, f32[128,1024]{1,0:T(8,128)S(1)}, u32[]{:S(2)}, u32[]{:S(2)}) collective-permute-start(f32[128,1024]{1,0:T(8,128)S(1)} %bitcast.44), channel_id=1, source_target_pairs={{0,32},{32,64},{64,96},{96,128},{128,160},{160,192},{192,224},{224... | collective-permute-start | bytes 1572872 | tf_op jit(solution)/shard_map/ppermute | solution.py:20
  121.5 0.7 copy-start
  134.6 12.2 %all-to-all-start.5 = ((bf16[16,8,1024]{2,1,0:T(8,128)(2,1)}), bf16[16,8,1024]{2,1,0:T(8,128)(2,1)S(1)}, u32[]{:S(2)}, u32[]{:S(2)}) async-start(bf16[16,8,1024]{2,1,0:T(8,128)(2,1)} %coarse_scan.3), calls=%async_computation.5 | async-start | bytes 524288 | tf_op jit(solution)/shard_map/all_to_all | solution.py:51
  140.4 87.4 %reduce-scatter.2.cloned.1.call-start = ((), (), s32[]{:S(2)}) async-start(), calls=%async_computation.7 | async-start | bytes 2228224 | tf_op jit(solution)/shard_map/reduce_scatter | solution.py:264
  146.8 1.0 copy-start.1
  151.1 6.1 %collective-permute-start.2 = (bf16[16,2,32,1024]{3,2,1,0:T(8,128)(2,1)S(1)}, bf16[16,2,32,1024]{3,2,1,0:T(8,128)(2,1)S(1)}, u32[]{:S(2)}, u32[]{:S(2)}) collective-permute-start(bf16[16,2,32,1024]{3,2,1,0:T(8,128)(2,1)S(1)} %get-tuple-element.36), channel_id=1, source_target_pairs={{0,1},{1,0},{2,3},{3,2},{4,5},{5,4},{6,7},{7,6},{8,9},{9,8},{10,11... | collective-permute-start | bytes 6291464 | tf_op jit(solution)/shard_map/ppermute | solution.py:254
  158.7 1.9 copy-start.6
  158.7 1.9 copy-start.7
  160.5 1.7 copy-start.4
  160.5 1.7 copy-start.5
  160.6 1.7 copy-start.8
Sparse Core Ops, SparseCore 0:
  10.1 77.7 all-gather.2
  158.8 69.0 reduce-scatter.1

commit v3 on v2

--- a/solution.py
+++ b/solution.py
@@ -20,14 +20,14 @@
     return lax.ppermute(block, axis, route)
 
 
-def scan_kernel(ends_ref, guess_ref, gains_ref, edge_ref, starts_ref, *, first, reverse):
-    blocks, rows = ends_ref.shape[:2]
+def scan_kernel(ends_ref, guess_ref, gains_ref, edge_ref, starts_ref, *, reverse):
+    blocks = ends_ref.shape[0]
     carry = jnp.zeros(ends_ref.shape[1:], f32)
     order = range(blocks - 1, -1, -1) if reverse else range(blocks)
     step = -1 if reverse else 1
     starts_ref[order[0]] = edge_ref[...]
     for k in order[:-1]:
-        guess = guess_ref[k, first : first + rows, :]
+        guess = guess_ref[k]
         resid = ends_ref[k].astype(f32) - guess
         carry = gains_ref[k : k + 1, :] * carry + resid
         starts_ref[k + step] = (guess + carry).astype(starts_ref.dtype)
@@ -39,9 +39,7 @@
     pieces = end.reshape(blocks, rows // blocks, width)
     mine = lax.all_to_all(pieces, "layer", 0, 0)
     starts = pl.pallas_call(
-        functools.partial(
-            scan_kernel, first=rows // blocks if reverse else 0, reverse=reverse
-        ),
+        functools.partial(scan_kernel, reverse=reverse),
         in_specs=[VMEM] * 4,
         out_specs=VMEM,
         out_shape=pltpu.VMEM(mine.shape, bf16),
@@ -213,22 +211,16 @@
     gains_all = lax.all_to_all(
         jnp.broadcast_to(gains[None], (count, 1, width)), "layer", 0, 0
     ).reshape(count, width)
-    guess_rows = lax.all_to_all(
-        jnp.concatenate(
-            [guess.reshape(count, own, width), lam.reshape(count, own, width)], 1
-        ),
-        "layer",
-        0,
-        0,
-    )
+    by_block = (count, own, width)
+    guess_rows = lax.all_to_all(guess.reshape(by_block), "layer", 0, 0)
+    lam_rows = lax.all_to_all(lam.reshape(by_block), "layer", 0, 0)
     anchor_rows = lax.dynamic_slice_in_dim(inputs, own * index, own)
     final_rows = lax.dynamic_slice_in_dim(cotangent, own * index, own)
     guess_start = jnp.where(index == 0, inputs.astype(f32), arrived)
     guess_end = jnp.where(index == count - 1, cotangent.astype(f32), arrived_adj)
-    guess_start, guess_end, gains_all, guess_rows, anchor_rows, final_rows = (
-        lax.optimization_barrier(
-            (guess_start, guess_end, gains_all, guess_rows, anchor_rows, final_rows)
-        )
+    held = (guess_start, guess_end, gains_all, guess_rows, lam_rows)
+    guess_start, guess_end, gains_all, guess_rows, lam_rows, anchor_rows, final_rows = (
+        lax.optimization_barrier((*held, anchor_rows, final_rows))
     )
     tall = (rows, width)
     relaxed, relaxed_low = call(
@@ -242,7 +234,7 @@
         [FAR(tall, f32), NEAR(later, bf16), NEAR(every, f32), FAR(tall, f32), NEAR(tall, bf16)],
         full_weights, (start, biases, guess_end),
     )
-    end_adj = corrected(back_low, guess_rows, gains_all, final_rows, True)
+    end_adj = corrected(back_low, lam_rows, gains_all, final_rows, True)
     core = lax.axis_index("c").astype(jnp.int32).reshape(1)
     chips, cores = lax.axis_size("z"), lax.axis_size("c")
     half = (chips, layers, width // (chips * cores), width)

time: 237 us -> 236 us (level)
  starting transfers between devices: 27.7 us -> 34.3 us
  other arithmetic: 7.25 us -> 2.97 us
    ppermute x2, waiting for transfers between devices: 17.7 us -> 0.01 us  [from_behind(): return lax.ppermute(block, axis, route)]
    all_to_all x1 -> x2, waiting for transfers between devices: 0.01 us -> 14.9 us  [the longest x1 8.01 us: local(): lam_rows = lax.all_to_all(lam.reshape(by_block), 'layer', 0, 0)]
    all_to_all x1 -> x2, starting transfers between devices: 5.51 us -> 11.3 us  [the longest x1 5.76 us: local(): lam_rows = lax.all_to_all(lam.reshape(by_block), 'layer', 0, 0)]
    all_gather x1, waiting for transfers between devices: 30.3 us -> 33.4 us  [local(): full_weights = lax.all_gather(weights, ('z', 'c'))]
    all_to_all x1, waiting for transfers between devices: 5.55 us -> 3.06 us  [local(): lax.all_to_all(jnp.broadcast_to(gains[None], (count, 1, width)), 'layer',...]
    concatenate x1 -> x0, other arithmetic: 2.38 us -> none  [local(): jnp.concatenate([guess.reshape(count, own, width), lam.reshape(count, own...]
  transfers between devices with their start and end apart: 8 -> 9, of which waited for: 6 -> 7; matrix products, arithmetic and copies ran while one was open for 5% -> 3% of each run, Pallas kernels for 0% -> 0%
where the time goes in v3:
time: 236 us; the launch traced here: 235 us
  waiting for transfers between devices  128 us (54%)
  blocking collectives  36.8 us (16%)
  starting transfers between devices  34.3 us (15%)
  between operations  14.2 us (6%)
  Pallas kernels  13.7 us (6%)
  local copies, waits for them, and re-layouts  4 us (2%)
  other arithmetic  2.97 us (1%)
    reduce_scatter x1, waiting for transfers between devices, local(): total = lax.psum_scatter(both, 'z', scatter_dimension=0, tiled=True)  65 us
    all_gather x1, waiting for transfers between devices, local(): full_weights = lax.all_gather(weights, ('z', 'c'))  33.4 us
    all_to_all x2, blocking collectives, corrected(): mine = lax.all_to_all(pieces, 'layer', 0, 0)  25.2 us
    all_to_all x1, blocking collectives, corrected(): return lax.all_to_all(starts, 'layer', 0, 0).reshape(rows, width)  11.6 us
    pallas_call x3, Pallas kernels, call(): pl.pallas_call(kernel, in_specs=[pl.BlockSpec(memory_space=pltpu.SMEM)] *...  11.3 us
    all_to_all x1, starting transfers between devices, local(): lax.all_to_all(jnp.broadcast_to(gains[None], (count, 1, width)), 'layer',...  9.13 us
    all_to_all x1, waiting for transfers between devices, local(): lam_rows = lax.all_to_all(lam.reshape(by_block), 'layer', 0, 0)  8.01 us
    all_to_all x1, waiting for transfers between devices, local(): guess_rows = lax.all_to_all(guess.reshape(by_block), 'layer', 0, 0)  6.93 us
  transfers between devices with their start and end apart: 9, of which 7 were waited for; matrix products, arithmetic and copies ran while one was open for 3% of the time, Pallas kernels for 0%

profile of v3, /device:TPU:6, one launch (start us, length us, event | category | flops | bytes accessed | tf_op | source)
XLA Modules:
  0.0 235.3 jit_solution(11909097396181679152)
XLA Ops:
  7.2 0.7 all-gather.3.cloned.1.call-update
  7.9 1.4 broadcast_in_dim.21
  9.3 9.1 %all-to-all-start = ((f32[16,1,1024]{2,1,0:T(1,128)}), f32[16,1,1024]{2,1,0:T(1,128)S(1)}, u32[]{:S(2)}, u32[]{:S(2)}) async-start(f32[16,1,1024]{2,1,0:T(1,128)} %broadcast_in_dim.21), calls=%async_computation | async-start | bytes 131072 | tf_op jit(solution)/shard_map/all_to_all | solution.py:211
  18.4 2.7 %collective-permute-start.1 = (f32[128,1024]{1,0:T(8,128)}, f32[128,1024]{1,0:T(8,128)S(1)}, u32[]{:S(2)}, u32[]{:S(2)}) collective-permute-start(f32[128,1024]{1,0:T(8,128)} %bitcast.43), channel_id=1, source_target_pairs={{32,0},{64,32},{96,64},{128,96},{160,128},{192,160},{224,192},{256... | collective-permute-start | bytes 1572872 | tf_op jit(solution)/shard_map/ppermute | solution.py:20
  21.2 3.1 %all-to-all-done = f32[16,1,1024]{2,1,0:T(1,128)S(1)} async-done(((f32[16,1,1024]{2,1,0:T(1,128)}), f32[16,1,1024]{2,1,0:T(1,128)S(1)}, u32[]{:S(2)}, u32[]{:S(2)}) %all-to-all-start) | async-done | bytes 65568 | tf_op jit(solution)/shard_map/all_to_all | solution.py:211
  24.2 5.5 %all-to-all-start.1 = ((f32[16,8,1024]{2,1,0:T(8,128)}), f32[16,8,1024]{2,1,0:T(8,128)S(1)}, u32[]{:S(2)}, u32[]{:S(2)}) async-start(f32[16,8,1024]{2,1,0:T(8,128)} %bitcast.41), calls=%async_computation.1 | async-start | bytes 1048576 | tf_op jit(solution)/shard_map/all_to_all | solution.py:215
  29.8 3.4 %collective-permute-start = (f32[128,1024]{1,0:T(8,128)}, f32[128,1024]{1,0:T(8,128)S(1)}, u32[]{:S(2)}, u32[]{:S(2)}) collective-permute-start(f32[128,1024]{1,0:T(8,128)} %bitcast.42), channel_id=1, source_target_pairs={{0,32},{32,64},{64,96},{96,128},{128,160},{160,192},{192,224},{224... | collective-permute-start | bytes 1572872 | tf_op jit(solution)/shard_map/ppermute | solution.py:20
  33.1 0.7 constant_dynamic-slice_fusion
  33.9 6.9 %all-to-all-done.1.guess_ref = f32[16,8,1024]{2,1,0:T(8,128)S(1)} async-done(((f32[16,8,1024]{2,1,0:T(8,128)}), f32[16,8,1024]{2,1,0:T(8,128)S(1)}, u32[]{:S(2)}, u32[]{:S(2)}) %all-to-all-start.1) | async-done | bytes 524320 | tf_op jit(solution)/shard_map/all_to_all | solution.py:215
  40.8 5.8 %all-to-all-start.2 = ((f32[16,8,1024]{2,1,0:T(8,128)}), f32[16,8,1024]{2,1,0:T(8,128)S(1)}, u32[]{:S(2)}, u32[]{:S(2)}) async-start(f32[16,8,1024]{2,1,0:T(8,128)} %bitcast.44), calls=%async_computation.2 | async-start | bytes 1048576 | tf_op jit(solution)/shard_map/all_to_all | solution.py:216
  46.6 0.1 convert_select_fusion.adj_ref
  46.7 0.1 convert_select_fusion.1.start_ref
  46.8 8.0 %all-to-all-done.2.guess_ref = f32[16,8,1024]{2,1,0:T(8,128)S(1)} async-done(((f32[16,8,1024]{2,1,0:T(8,128)}), f32[16,8,1024]{2,1,0:T(8,128)S(1)}, u32[]{:S(2)}, u32[]{:S(2)}) %all-to-all-start.2) | async-done | bytes 524320 | tf_op jit(solution)/shard_map/all_to_all | solution.py:216
  54.8 33.4 %all-gather.3.cloned.1.call-done = bf16[64,32,1024]{2,1,0:T(8,128)(2,1)} async-done(((bf16[2,32,1024]{2,1,0:T(8,128)(2,1)}), bf16[64,32,1024]{2,1,0:T(8,128)(2,1)}) %all-gather.3.cloned.1.call-update) | async-done | bytes 4194320 | tf_op jit(solution)/shard_map/all_gather | solution.py:201
  88.2 3.3 %relax.1 = (f32[128,1024]{1,0:T(8,128)}, bf16[128,1024]{1,0:T(8,128)(2,1)S(1)}) custom-call(bf16[32,2,32,1024]{3,2,1,0:T(8,128)(2,1)} %bitcast.36, f32[128,1024]{1,0:T(8,128)S(1)} %convert_select_fusion.1.start_ref, f32[2,1024]{1,0:T(2,128)S(1)} %copy-done), custom_call_target="tpu_custom_call" | custom-call | tf_op jit(solution)/shard_map/relax/pallas_call | solution.py:184
  91.5 13.7 %all_to_all.35.ends_ref = bf16[16,8,1024]{2,1,0:T(8,128)(2,1)S(1)} all-to-all(bf16[16,8,1024]{2,1,0:T(8,128)(2,1)S(1)} %bitcast.35), channel_id=1, replica_groups=mesh['layer'=16,'z'=16,'c'=2] {'layer'}, dimensions={0} | all-to-all | bytes 524288 | tf_op jit(solution)/shard_map/all_to_all | solution.py:40
  105.1 0.1 coarse_scan.2
  105.2 11.6 %all_to_all.36 = bf16[16,8,1024]{2,1,0:T(8,128)(2,1)S(1)} all-to-all(bf16[16,8,1024]{2,1,0:T(8,128)(2,1)S(1)} %coarse_scan.2), channel_id=1, replica_groups=mesh['layer'=16,'z'=16,'c'=2] {'layer'}, dimensions={0} | all-to-all | bytes 524288 | tf_op jit(solution)/shard_map/all_to_all | solution.py:49
  116.8 4.7 %both_ways.1 = (f32[128,1024]{1,0:T(8,128)}, bf16[1,128,1024]{2,1,0:T(8,128)(2,1)S(1)}, f32[2,128,1024]{2,1,0:T(8,128)S(1)}, f32[128,1024]{1,0:T(8,128)}, bf16[128,1024]{1,0:T(8,128)(2,1)S(1)}) custom-call(bf16[32,2,32,1024]{3,2,1,0:T(8,128)(2,1)} %bitcast.37, bf16[128,1024]{1,0:T(8,128)(2,1)S(1)} %bitcast.29, f32[2,1024]{1,0:T(2,128)S(1)} %copy-done, ...), custom_call_target="tpu_custom_call" | custom-call | tf_op jit(solution)/shard_map/both_ways/pallas_call | solution.py:184
  121.5 11.6 %all_to_all.37.ends_ref = bf16[16,8,1024]{2,1,0:T(8,128)(2,1)S(1)} all-to-all(bf16[16,8,1024]{2,1,0:T(8,128)(2,1)S(1)} %bitcast.34), channel_id=1, replica_groups=mesh['layer'=16,'z'=16,'c'=2] {'layer'}, dimensions={0} | all-to-all | bytes 524288 | tf_op jit(solution)/shard_map/all_to_all | solution.py:40
  133.1 0.8 coarse_scan.3
  133.9 5.8 %all-to-all-start.6 = ((bf16[16,8,1024]{2,1,0:T(8,128)(2,1)}), bf16[16,8,1024]{2,1,0:T(8,128)(2,1)S(1)}, u32[]{:S(2)}, u32[]{:S(2)}) async-start(bf16[16,8,1024]{2,1,0:T(8,128)(2,1)} %coarse_scan.3), calls=%async_computation.6 | async-start | bytes 524288 | tf_op jit(solution)/shard_map/all_to_all | solution.py:49
  139.8 6.3 %all-to-all-done.6 = bf16[16,8,1024]{2,1,0:T(8,128)(2,1)S(1)} async-done(((bf16[16,8,1024]{2,1,0:T(8,128)(2,1)}), bf16[16,8,1024]{2,1,0:T(8,128)(2,1)S(1)}, u32[]{:S(2)}, u32[]{:S(2)}) %all-to-all-start.6) | async-done | bytes 262176 | tf_op jit(solution)/shard_map/all_to_all | solution.py:49
  146.1 3.4 %grads.1 = (bf16[16,2,32,1024]{3,2,1,0:T(8,128)(2,1)S(1)}, bf16[16,2,32,1024]{3,2,1,0:T(8,128)(2,1)S(1)}, f32[128,1024]{1,0:T(8,128)}, bf16[128,1024]{1,0:T(8,128)(2,1)}) custom-call(s32[1]{0:T(128)} %bitcast.9.core_ref, bf16[32,2,32,1024]{3,2,1,0:T(8,128)(2,1)} %bitcast.38, bf16[128,1024]{1,0:T(8,128)(2,1)S(1)} %bitcast.31, ...), custom_call_target="tpu_custom_call" | custom-call | tf_op jit(solution)/shard_map/grads/pallas_call | solution.py:184
  149.5 1.9 collective-permute-start.2
  151.4 4.1 %collective-permute-done.2.theirs_ref = bf16[16,2,32,1024]{3,2,1,0:T(8,128)(2,1)S(1)} collective-permute-done((bf16[16,2,32,1024]{3,2,1,0:T(8,128)(2,1)S(1)}, bf16[16,2,32,1024]{3,2,1,0:T(8,128)(2,1)S(1)}, u32[]{:S(2)}, u32[]{:S(2)}) %collective-permute-start.2) | collective-permute-done | bytes 2097184 | tf_op jit(solution)/shard_map/ppermute | solution.py:246
  155.6 1.4 add_halves.1
  157.1 1.8 slice.4
  159.0 1.6 fusion.1
  160.6 1.2 add_bitcast_fusion
  161.8 65.0 %reduce-scatter.2.cloned.1.call-done = bf16[1,2,32,1024]{3,2,1,0:T(8,128)(2,1)} async-done(((bf16[16,2,32,1024]{3,2,1,0:T(8,128)(2,1)}), bf16[1,2,32,1024]{3,2,1,0:T(8,128)(2,1)}) %reduce-scatter.2.cloned.1.call-update) | async-done | bytes 131088 | tf_op jit(solution)/shard_map/reduce_scatter | solution.py:256
  226.8 1.6 bitcast_convert_fusion
  (22 shorter events, 0.2 us)
Async XLA Ops:
  7.2 39.4 %copy-start.4 = (bf16[128,1024]{1,0:T(8,128)(2,1)S(1)}, bf16[128,1024]{1,0:T(8,128)(2,1)}, u32[]{:S(2)}) copy-start(bf16[128,1024]{1,0:T(8,128)(2,1)} %param.13) | copy-start | bytes 786436
  7.2 39.5 %copy-start.5 = (bf16[128,1024]{1,0:T(8,128)(2,1)S(1)}, bf16[128,1024]{1,0:T(8,128)(2,1)}, u32[]{:S(2)}) copy-start(bf16[128,1024]{1,0:T(8,128)(2,1)} %param.7) | copy-start | bytes 786436
  7.2 81.0 %all-gather.3.cloned.1.call-start = ((), (), s32[]{:S(2)}) async-start(), calls=%async_computation.9 | async-start | bytes 4325376 | tf_op jit(solution)/shard_map/all_gather | solution.py:201
  9.3 14.9 %all-to-all-start = ((f32[16,1,1024]{2,1,0:T(1,128)}), f32[16,1,1024]{2,1,0:T(1,128)S(1)}, u32[]{:S(2)}, u32[]{:S(2)}) async-start(f32[16,1,1024]{2,1,0:T(1,128)} %broadcast_in_dim.21), calls=%async_computation | async-start | bytes 131072 | tf_op jit(solution)/shard_map/all_to_all | solution.py:211
  18.4 28.2 %collective-permute-start.1 = (f32[128,1024]{1,0:T(8,128)}, f32[128,1024]{1,0:T(8,128)S(1)}, u32[]{:S(2)}, u32[]{:S(2)}) collective-permute-start(f32[128,1024]{1,0:T(8,128)} %bitcast.43), channel_id=1, source_target_pairs={{32,0},{64,32},{96,64},{128,96},{160,128},{192,160},{224,192},{256... | collective-permute-start | bytes 1572872 | tf_op jit(solution)/shard_map/ppermute | solution.py:20
  24.2 16.6 %all-to-all-start.1 = ((f32[16,8,1024]{2,1,0:T(8,128)}), f32[16,8,1024]{2,1,0:T(8,128)S(1)}, u32[]{:S(2)}, u32[]{:S(2)}) async-start(f32[16,8,1024]{2,1,0:T(8,128)} %bitcast.41), calls=%async_computation.1 | async-start | bytes 1048576 | tf_op jit(solution)/shard_map/all_to_all | solution.py:215
  29.7 58.4 %copy-start = (f32[2,1024]{1,0:T(2,128)S(1)}, f32[2,1024]{1,0:T(2,128)}, u32[]{:S(2)}) copy-start(f32[2,1024]{1,0:T(2,128)} %b_ref.3) | copy-start | bytes 24580
  29.8 16.9 %collective-permute-start = (f32[128,1024]{1,0:T(8,128)}, f32[128,1024]{1,0:T(8,128)S(1)}, u32[]{:S(2)}, u32[]{:S(2)}) collective-permute-start(f32[128,1024]{1,0:T(8,128)} %bitcast.42), channel_id=1, source_target_pairs={{0,32},{32,64},{64,96},{96,128},{128,160},{160,192},{192,224},{224... | collective-permute-start | bytes 1572872 | tf_op jit(solution)/shard_map/ppermute | solution.py:20
  40.8 13.9 %all-to-all-start.2 = ((f32[16,8,1024]{2,1,0:T(8,128)}), f32[16,8,1024]{2,1,0:T(8,128)S(1)}, u32[]{:S(2)}, u32[]{:S(2)}) async-start(f32[16,8,1024]{2,1,0:T(8,128)} %bitcast.44), calls=%async_computation.2 | async-start | bytes 1048576 | tf_op jit(solution)/shard_map/all_to_all | solution.py:216
  133.9 12.2 %all-to-all-start.6 = ((bf16[16,8,1024]{2,1,0:T(8,128)(2,1)}), bf16[16,8,1024]{2,1,0:T(8,128)(2,1)S(1)}, u32[]{:S(2)}, u32[]{:S(2)}) async-start(bf16[16,8,1024]{2,1,0:T(8,128)(2,1)} %coarse_scan.3), calls=%async_computation.6 | async-start | bytes 524288 | tf_op jit(solution)/shard_map/all_to_all | solution.py:49
  139.8 87.1 %reduce-scatter.2.cloned.1.call-start = ((), (), s32[]{:S(2)}) async-start(), calls=%async_computation.8 | async-start | bytes 2228224 | tf_op jit(solution)/shard_map/reduce_scatter | solution.py:256
  149.5 6.1 %collective-permute-start.2 = (bf16[16,2,32,1024]{3,2,1,0:T(8,128)(2,1)S(1)}, bf16[16,2,32,1024]{3,2,1,0:T(8,128)(2,1)S(1)}, u32[]{:S(2)}, u32[]{:S(2)}) collective-permute-start(bf16[16,2,32,1024]{3,2,1,0:T(8,128)(2,1)S(1)} %get-tuple-element.38), channel_id=1, source_target_pairs={{0,1},{1,0},{2,3},{3,2},{4,5},{5,4},{6,7},{7,6},{8,9},{9,8},{10,11... | collective-permute-start | bytes 6291464 | tf_op jit(solution)/shard_map/ppermute | solution.py:246
  157.0 1.9 copy-start.3
  157.0 1.9 copy-start.6
  158.9 1.7 copy-start.1
  158.9 1.7 copy-start.2
  158.9 1.7 copy-start.7
Sparse Core Ops, SparseCore 0:
  10.1 78.0 all-gather.2
  157.2 69.6 reduce-scatter.1

commit v4 on v3

--- a/solution.py
+++ b/solution.py
@@ -121,53 +121,52 @@
     rounded_ref[...] = adjoint.astype(bf16)
 
 
-def grads_kernel(
-    core_ref, w_ref, adj_ref, slopes_ref, start_ref, kept_ref,
-    mine_ref, theirs_ref, adj_out_ref, scaled_ref, held, sems,
+def scaled_kernel(
+    w_ref, adj_ref, slopes_ref, start_ref, kept_ref, send_ref, held, sems
 ):
     layers, bands = sems.shape
-    chips, _, rows, width = mine_ref.shape
-    copies = fetch(w_ref, held, sems, range(1, layers))
+    copies = fetch(w_ref, held, sems, range(layers - 1, 0, -1))
+    send_ref[0] = start_ref[...]
+    for l in range(1, layers):
+        send_ref[l] = kept_ref[l - 1]
+    adjoint = adj_ref[...].astype(f32)
+    send_ref[2 * layers - 1] = (adjoint * slopes_ref[layers - 1]).astype(bf16)
+    size = held.shape[1] // bands
+    for l in range(layers - 1, 0, -1):
+        scaled = send_ref[layers + l]
+        parts = []
+        for n in range(bands):
+            copies[l, n].wait()
+            weight = square(held[l, n * size : (n + 1) * size])
+            tall = weight.shape[0]
+            at = slice(n * tall, (n + 1) * tall)
+            parts.append(adjoint[:, at] + back_step(scaled, weight))
+            send_ref[layers + l - 1, :, at] = (
+                parts[n] * slopes_ref[l - 1, :, at]
+            ).astype(bf16)
+        if l > 1:
+            adjoint = jnp.concatenate(parts, 1)
+
+
+def grads_kernel(core_ref, mine_ref, theirs_ref, both_ref, picked, sums, sems):
+    layers = sums.shape[1]
+    chips, _, rows, width = sums.shape
     first = core_ref[0] == 0
-    parts = 4
-    adjoint = adj_ref[...].astype(f32)
-    for l in reversed(range(layers)):
-        scaled = (adjoint * slopes_ref[l]).astype(bf16)
-        size = width // parts
-        for m in range(parts):
-            columns = slice(m * size, (m + 1) * size)
-            kept = kept_ref[l - 1, :, columns] if l else start_ref[:, columns]
-            grad = step_size * lax.dot_general(
-                kept,
-                scaled,
-                (((0,), (0,)), ((), ())),
-                preferred_element_type=f32,
+    deep = mine_ref.shape[1]
+    copies = []
+    for l in range(layers):
+        for at, ref in ((0, mine_ref), (deep, theirs_ref)):
+            turned = ref[l].T.reshape(chips, 2, rows, deep)
+            picked[:, at : at + deep] = square(
+                jnp.where(first, turned[:, 0], turned[:, 1])
             )
-            grad = grad.reshape(chips // parts, 2, rows, width)
-            at = slice(m * chips // parts, (m + 1) * chips // parts)
-            zero, one = grad[:, 0], grad[:, 1]
-            mine_ref[at, l] = jnp.where(first, zero, one).astype(bf16)
-            theirs_ref[at, l] = jnp.where(first, one, zero).astype(bf16)
-        if l:
-            for n in range(bands):
-                copies[l, n].wait()
-            adjoint = adjoint + back_step(scaled, square(held[l]))
-        else:
-            adj_out_ref[...] = adjoint
-            scaled_ref[...] = scaled
-
-
-def add_kernel(mine_ref, theirs_ref, both_ref, sums, sems):
-    copies = []
-    parts = sems.shape[0]
-    size = sums.shape[0] // parts
-    for n in range(parts):
-        part = pl.ds(n * size, size)
-        sums[part] = mine_ref[part] + theirs_ref[part]
+        scaled = jnp.concatenate([mine_ref[layers + l], theirs_ref[layers + l]], 0)
+        grad = step_size * jnp.dot(picked[...], scaled, preferred_element_type=f32)
+        sums[:, l] = grad.reshape(chips, rows, width).astype(bf16)
         copies.append(
-            pltpu.make_async_copy(sums.at[part], both_ref.at[part], sems.at[n])
+            pltpu.make_async_copy(sums.at[:, l], both_ref.at[:, l], sems.at[l])
         )
-        copies[n].start()
+        copies[l].start()
     for copy in copies:
         copy.wait()
 
@@ -179,13 +178,11 @@
 FAR, NEAR = pltpu.HBM, pltpu.VMEM
 
 
-def call(kernel, name, outs, weights, ins, bands=4, scalars=()):
+def call(kernel, name, outs, weights, ins, bands=4):
     count, layers, rows, width = weights.shape
     return pl.pallas_call(
         kernel,
-        in_specs=[pl.BlockSpec(memory_space=pltpu.SMEM)] * len(scalars)
-        + [pl.BlockSpec(memory_space=pl.ANY)]
-        + [VMEM] * len(ins),
+        in_specs=[pl.BlockSpec(memory_space=pl.ANY)] + [VMEM] * len(ins),
         out_specs=[VMEM] * len(outs),
         out_shape=outs,
         scratch_shapes=[
@@ -194,7 +191,7 @@
         ],
         compiler_params=SMALL,
         name=name,
-    )(*scalars, pltpu.with_memory_space_constraint(weights, pltpu.HBM), *map(near, ins))
+    )(pltpu.with_memory_space_constraint(weights, pltpu.HBM), *map(near, ins))
 
 
 def local(inputs, guess_fwd, guess_adj, weights, biases, gains, cotangent):
@@ -237,24 +234,29 @@
     end_adj = corrected(back_low, lam_rows, gains_all, final_rows, True)
     core = lax.axis_index("c").astype(jnp.int32).reshape(1)
     chips, cores = lax.axis_size("z"), lax.axis_size("c")
-    half = (chips, layers, width // (chips * cores), width)
-    mine, theirs, adjoint, scaled = call(
-        grads_kernel, "grads",
-        [NEAR(half, bf16), NEAR(half, bf16), FAR(tall, f32), FAR(tall, bf16)],
-        full_weights, (end_adj, slopes, start, kept), scalars=(core,),
-    )
-    theirs = lax.ppermute(theirs, "c", [(0, 1), (1, 0)])
+    part = (chips, layers, width // (chips * cores), width)
+    (mine,) = call(
+        scaled_kernel, "scaled", [NEAR((2 * layers, rows, width), bf16)],
+        full_weights, (end_adj, slopes, start, kept),
+    )
+    theirs = lax.ppermute(mine, "c", [(0, 1), (1, 0)])
     both = pl.pallas_call(
-        add_kernel,
-        in_specs=[VMEM] * 2,
+        grads_kernel,
+        in_specs=[pl.BlockSpec(memory_space=pltpu.SMEM), VMEM, VMEM],
         out_specs=pl.BlockSpec(memory_space=pl.ANY),
-        out_shape=jax.ShapeDtypeStruct(half, bf16),
-        scratch_shapes=[pltpu.VMEM(half, bf16), pltpu.SemaphoreType.DMA((4,))],
+        out_shape=FAR(part, bf16),
+        scratch_shapes=[
+            pltpu.VMEM((width // cores, cores * rows), bf16),
+            pltpu.VMEM(part, bf16),
+            pltpu.SemaphoreType.DMA((layers,)),
+        ],
         compiler_params=SMALL,
-        name="add_halves",
-    )(near(mine), near(theirs))
+        name="grads",
+    )(core, near(mine), near(theirs))
     total = lax.psum_scatter(both, "z", scatter_dimension=0, tiled=True)
-    adjoint = adjoint + back_step(scaled, square(full_weights[:, 0]))
+    adjoint = end_adj.astype(f32)
+    for l in reversed(range(layers)):
+        adjoint = adjoint + back_step(mine[layers + l], square(full_weights[:, l]))
     coarse = relaxed + gains * (start.astype(f32) - guess_start)
     coarse_adj = back + gains * (end_adj.astype(f32) - guess_end)
     return (

time: 236 us -> 234 us (level)
  blocking collectives: 36.8 us -> 48.4 us
  waiting for transfers between devices: 128 us -> 118 us
  starting transfers between devices: 34.3 us -> 28.5 us
    all_to_all x1 -> x2, blocking collectives: 11.6 us -> 23.2 us  [corrected(): return lax.all_to_all(starts, 'layer', 0, 0).reshape(rows, width)]
    all_to_all x1 -> x0, waiting for transfers between devices: 6.3 us -> none  [corrected(): return lax.all_to_all(starts, 'layer', 0, 0).reshape(rows, width)]
    all_to_all x1 -> x0, starting transfers between devices: 5.81 us -> none  [corrected(): return lax.all_to_all(starts, 'layer', 0, 0).reshape(rows, width)]
  transfers between devices with their start and end apart: 9 -> 8, of which waited for: 7 -> 6; matrix products, arithmetic and copies ran while one was open for 3% -> 4% of each run, Pallas kernels for 0% -> 0%
where the time goes in v4:
time: 234 us
  waiting for transfers between devices  118 us (50%)
  blocking collectives  48.4 us (21%)
  starting transfers between devices  28.5 us (12%)
  between operations  14.2 us (6%)
  Pallas kernels  14.1 us (6%)
  local copies, waits for them, and re-layouts  4.82 us (2%)
  other arithmetic  2.98 us (1%)
  matrix products  2.51 us (1%)
    reduce_scatter x1, waiting for transfers between devices, local(): total = lax.psum_scatter(both, 'z', scatter_dimension=0, tiled=True)  63.1 us
    all_gather x1, waiting for transfers between devices, local(): full_weights = lax.all_gather(weights, ('z', 'c'))  33.4 us
    all_to_all x2, blocking collectives, corrected(): mine = lax.all_to_all(pieces, 'layer', 0, 0)  25.2 us
    all_to_all x2, blocking collectives, corrected(): return lax.all_to_all(starts, 'layer', 0, 0).reshape(rows, width)  23.2 us
    pallas_call x3, Pallas kernels, call(): pl.pallas_call(kernel, in_specs=[pl.BlockSpec(memory_space=pl.ANY)] + [VM...  10.8 us
    all_to_all x1, starting transfers between devices, local(): lax.all_to_all(jnp.broadcast_to(gains[None], (count, 1, width)), 'layer',...  9.13 us
    all_to_all x1, waiting for transfers between devices, local(): guess_rows = lax.all_to_all(guess.reshape(by_block), 'layer', 0, 0)  7.96 us
    all_to_all x1, waiting for transfers between devices, local(): lam_rows = lax.all_to_all(lam.reshape(by_block), 'layer', 0, 0)  6.93 us
  transfers between devices with their start and end apart: 8, of which 6 were waited for; matrix products, arithmetic and copies ran while one was open for 4% of the time, Pallas kernels for 0%

profile of v4, /device:TPU:6, one launch (start us, length us, event | category | flops | bytes accessed | tf_op | source)
XLA Modules:
  0.0 233.5 jit_solution(632758013509591144)
XLA Ops:
  7.2 0.7 all-gather.3.cloned.1.call-update
  7.9 1.4 broadcast_in_dim.21
  9.3 9.1 %all-to-all-start = ((f32[16,1,1024]{2,1,0:T(1,128)}), f32[16,1,1024]{2,1,0:T(1,128)S(1)}, u32[]{:S(2)}, u32[]{:S(2)}) async-start(f32[16,1,1024]{2,1,0:T(1,128)} %broadcast_in_dim.21), calls=%async_computation | async-start | bytes 131072 | tf_op jit(solution)/shard_map/all_to_all | solution.py:208
  18.4 2.7 %collective-permute-start.1 = (f32[128,1024]{1,0:T(8,128)}, f32[128,1024]{1,0:T(8,128)S(1)}, u32[]{:S(2)}, u32[]{:S(2)}) collective-permute-start(f32[128,1024]{1,0:T(8,128)} %bitcast.50), channel_id=1, source_target_pairs={{32,0},{64,32},{96,64},{128,96},{160,128},{192,160},{224,192},{256... | collective-permute-start | bytes 1572872 | tf_op jit(solution)/shard_map/ppermute | solution.py:20
  21.2 3.1 %all-to-all-done = f32[16,1,1024]{2,1,0:T(1,128)S(1)} async-done(((f32[16,1,1024]{2,1,0:T(1,128)}), f32[16,1,1024]{2,1,0:T(1,128)S(1)}, u32[]{:S(2)}, u32[]{:S(2)}) %all-to-all-start) | async-done | bytes 65568 | tf_op jit(solution)/shard_map/all_to_all | solution.py:208
  24.2 5.5 %all-to-all-start.2 = ((f32[16,8,1024]{2,1,0:T(8,128)}), f32[16,8,1024]{2,1,0:T(8,128)S(1)}, u32[]{:S(2)}, u32[]{:S(2)}) async-start(f32[16,8,1024]{2,1,0:T(8,128)} %bitcast.51), calls=%async_computation.2 | async-start | bytes 1048576 | tf_op jit(solution)/shard_map/all_to_all | solution.py:213
  29.8 3.4 %collective-permute-start = (f32[128,1024]{1,0:T(8,128)}, f32[128,1024]{1,0:T(8,128)S(1)}, u32[]{:S(2)}, u32[]{:S(2)}) collective-permute-start(f32[128,1024]{1,0:T(8,128)} %bitcast.52), channel_id=1, source_target_pairs={{0,32},{32,64},{64,96},{96,128},{128,160},{160,192},{192,224},{224... | collective-permute-start | bytes 1572872 | tf_op jit(solution)/shard_map/ppermute | solution.py:20
  33.1 0.7 constant_dynamic-slice_fusion
  33.9 6.9 %all-to-all-done.2.guess_ref = f32[16,8,1024]{2,1,0:T(8,128)S(1)} async-done(((f32[16,8,1024]{2,1,0:T(8,128)}), f32[16,8,1024]{2,1,0:T(8,128)S(1)}, u32[]{:S(2)}, u32[]{:S(2)}) %all-to-all-start.2) | async-done | bytes 524320 | tf_op jit(solution)/shard_map/all_to_all | solution.py:213
  40.8 5.8 %all-to-all-start.1 = ((f32[16,8,1024]{2,1,0:T(8,128)}), f32[16,8,1024]{2,1,0:T(8,128)S(1)}, u32[]{:S(2)}, u32[]{:S(2)}) async-start(f32[16,8,1024]{2,1,0:T(8,128)} %bitcast.53), calls=%async_computation.1 | async-start | bytes 1048576 | tf_op jit(solution)/shard_map/all_to_all | solution.py:212
  46.7 0.1 convert_select_fusion.adj_ref
  46.8 0.1 convert_select_fusion.1.start_ref
  46.8 8.0 %all-to-all-done.1.guess_ref = f32[16,8,1024]{2,1,0:T(8,128)S(1)} async-done(((f32[16,8,1024]{2,1,0:T(8,128)}), f32[16,8,1024]{2,1,0:T(8,128)S(1)}, u32[]{:S(2)}, u32[]{:S(2)}) %all-to-all-start.1) | async-done | bytes 524320 | tf_op jit(solution)/shard_map/all_to_all | solution.py:212
  54.8 33.4 %all-gather.3.cloned.1.call-done = bf16[64,32,1024]{2,1,0:T(8,128)(2,1)} async-done(((bf16[2,32,1024]{2,1,0:T(8,128)(2,1)}), bf16[64,32,1024]{2,1,0:T(8,128)(2,1)}) %all-gather.3.cloned.1.call-update) | async-done | bytes 4194320 | tf_op jit(solution)/shard_map/all_gather | solution.py:198
  88.2 3.3 %relax.1 = (f32[128,1024]{1,0:T(8,128)}, bf16[128,1024]{1,0:T(8,128)(2,1)S(1)}) custom-call(bf16[32,2,32,1024]{3,2,1,0:T(8,128)(2,1)} %bitcast.44, f32[128,1024]{1,0:T(8,128)S(1)} %convert_select_fusion.1.start_ref, f32[2,1024]{1,0:T(2,128)S(1)} %copy-done), custom_call_target="tpu_custom_call" | custom-call | tf_op jit(solution)/shard_map/relax/pallas_call | solution.py:183
  91.5 13.7 %all_to_all.35.ends_ref = bf16[16,8,1024]{2,1,0:T(8,128)(2,1)S(1)} all-to-all(bf16[16,8,1024]{2,1,0:T(8,128)(2,1)S(1)} %bitcast.43), channel_id=1, replica_groups=mesh['layer'=16,'z'=16,'c'=2] {'layer'}, dimensions={0} | all-to-all | bytes 524288 | tf_op jit(solution)/shard_map/all_to_all | solution.py:40
  105.1 0.1 coarse_scan.2
  105.2 11.6 %all_to_all.36 = bf16[16,8,1024]{2,1,0:T(8,128)(2,1)S(1)} all-to-all(bf16[16,8,1024]{2,1,0:T(8,128)(2,1)S(1)} %coarse_scan.2), channel_id=1, replica_groups=mesh['layer'=16,'z'=16,'c'=2] {'layer'}, dimensions={0} | all-to-all | bytes 524288 | tf_op jit(solution)/shard_map/all_to_all | solution.py:49
  116.8 4.7 %both_ways.1 = (f32[128,1024]{1,0:T(8,128)}, bf16[1,128,1024]{2,1,0:T(8,128)(2,1)S(1)}, f32[2,128,1024]{2,1,0:T(8,128)S(1)}, f32[128,1024]{1,0:T(8,128)}, bf16[128,1024]{1,0:T(8,128)(2,1)S(1)}) custom-call(bf16[32,2,32,1024]{3,2,1,0:T(8,128)(2,1)} %bitcast.45, bf16[128,1024]{1,0:T(8,128)(2,1)S(1)} %bitcast.37, f32[2,1024]{1,0:T(2,128)S(1)} %copy-done, ...), custom_call_target="tpu_custom_call" | custom-call | tf_op jit(solution)/shard_map/both_ways/pallas_call | solution.py:183
  121.5 11.6 %all_to_all.37.ends_ref = bf16[16,8,1024]{2,1,0:T(8,128)(2,1)S(1)} all-to-all(bf16[16,8,1024]{2,1,0:T(8,128)(2,1)S(1)} %bitcast.42), channel_id=1, replica_groups=mesh['layer'=16,'z'=16,'c'=2] {'layer'}, dimensions={0} | all-to-all | bytes 524288 | tf_op jit(solution)/shard_map/all_to_all | solution.py:40
  133.1 0.1 coarse_scan.3
  133.2 11.6 %all_to_all.38 = bf16[16,8,1024]{2,1,0:T(8,128)(2,1)S(1)} all-to-all(bf16[16,8,1024]{2,1,0:T(8,128)(2,1)S(1)} %coarse_scan.3), channel_id=1, replica_groups=mesh['layer'=16,'z'=16,'c'=2] {'layer'}, dimensions={0} | all-to-all | bytes 524288 | tf_op jit(solution)/shard_map/all_to_all | solution.py:49
  144.8 2.8 %scaled.1.mine_ref = bf16[4,128,1024]{2,1,0:T(8,128)(2,1)S(1)} custom-call(bf16[32,2,32,1024]{3,2,1,0:T(8,128)(2,1)} %bitcast.46, bf16[128,1024]{1,0:T(8,128)(2,1)S(1)} %bitcast.39, f32[2,128,1024]{2,1,0:T(8,128)S(1)} %get-tuple-element.29.slopes_ref, bf16[128,1024]{1,0:T(8,128)(2,1)S(1)} %bitcast.38, bf16[1,128,1024]{2,1,0:T(8,128)(2,1)S(1)} %get-tuple-element.30.kept_ref), custom_call_target="tpu_custom_call" | custom-call | tf_op jit(solution)/shard_map/scaled/pallas_call | solution.py:183
  147.6 1.9 collective-permute-start.2
  149.6 2.8 %collective-permute-done.2.theirs_ref = bf16[4,128,1024]{2,1,0:T(8,128)(2,1)} collective-permute-done((bf16[4,128,1024]{2,1,0:T(8,128)(2,1)S(1)}, bf16[4,128,1024]{2,1,0:T(8,128)(2,1)}, u32[]{:S(2)}, u32[]{:S(2)}) %collective-permute-start.2) | collective-permute-done | bytes 1048608 | tf_op jit(solution)/shard_map/ppermute | solution.py:242
  152.3 3.1 %grads.1 = bf16[16,2,32,1024]{3,2,1,0:T(8,128)(2,1)} custom-call(s32[1]{0:T(128)} %bitcast.16.core_ref, bf16[4,128,1024]{2,1,0:T(8,128)(2,1)S(1)} %scaled.1.mine_ref, bf16[4,128,1024]{2,1,0:T(8,128)(2,1)} %collective-permute-done.2.theirs_ref), custom_call_target="tpu_custom_call" | custom-call | tf_op jit(solution)/shard_map/grads/pallas_call | solution.py:243
  155.5 2.7 %fusion.6 = (bf16[32,1,32,1024]{3,2,1,0:T(8,128)(2,1)S(1)}, bf16[32,1,32,1024]{3,2,1,0:T(8,128)(2,1)S(1)}) fusion(bf16[32,2,32,1024]{3,2,1,0:T(8,128)(2,1)} %bitcast.47), kind=kLoop, calls=%fused_computation.18 | loop fusion | bytes 8388608 | tf_op jit(solution)/shard_map/slice | solution.py:259
  158.2 0.9 fusion.2
  159.1 1.6 fusion.1
  160.7 1.2 fusion.5
  161.9 63.1 %reduce-scatter.2.cloned.1.call-done = bf16[1,2,32,1024]{3,2,1,0:T(8,128)(2,1)} async-done(((bf16[16,2,32,1024]{3,2,1,0:T(8,128)(2,1)}), bf16[1,2,32,1024]{3,2,1,0:T(8,128)(2,1)}) %reduce-scatter.2.cloned.1.call-update) | async-done | bytes 131088 | tf_op jit(solution)/shard_map/reduce_scatter | solution.py:256
  225.1 1.6 bitcast_convert_fusion
  (18 shorter events, 0.1 us)
Async XLA Ops:
  7.2 39.5 %copy-start.3 = (bf16[128,1024]{1,0:T(8,128)(2,1)S(1)}, bf16[128,1024]{1,0:T(8,128)(2,1)}, u32[]{:S(2)}) copy-start(bf16[128,1024]{1,0:T(8,128)(2,1)} %param.13) | copy-start | bytes 786436
  7.2 39.6 %copy-start.4 = (bf16[128,1024]{1,0:T(8,128)(2,1)S(1)}, bf16[128,1024]{1,0:T(8,128)(2,1)}, u32[]{:S(2)}) copy-start(bf16[128,1024]{1,0:T(8,128)(2,1)} %param.7) | copy-start | bytes 786436
  7.2 81.0 %all-gather.3.cloned.1.call-start = ((), (), s32[]{:S(2)}) async-start(), calls=%async_computation.9 | async-start | bytes 4325376 | tf_op jit(solution)/shard_map/all_gather | solution.py:198
  9.3 14.9 %all-to-all-start = ((f32[16,1,1024]{2,1,0:T(1,128)}), f32[16,1,1024]{2,1,0:T(1,128)S(1)}, u32[]{:S(2)}, u32[]{:S(2)}) async-start(f32[16,1,1024]{2,1,0:T(1,128)} %broadcast_in_dim.21), calls=%async_computation | async-start | bytes 131072 | tf_op jit(solution)/shard_map/all_to_all | solution.py:208
  18.4 28.2 %collective-permute-start.1 = (f32[128,1024]{1,0:T(8,128)}, f32[128,1024]{1,0:T(8,128)S(1)}, u32[]{:S(2)}, u32[]{:S(2)}) collective-permute-start(f32[128,1024]{1,0:T(8,128)} %bitcast.50), channel_id=1, source_target_pairs={{32,0},{64,32},{96,64},{128,96},{160,128},{192,160},{224,192},{256... | collective-permute-start | bytes 1572872 | tf_op jit(solution)/shard_map/ppermute | solution.py:20
  24.2 16.6 %all-to-all-start.2 = ((f32[16,8,1024]{2,1,0:T(8,128)}), f32[16,8,1024]{2,1,0:T(8,128)S(1)}, u32[]{:S(2)}, u32[]{:S(2)}) async-start(f32[16,8,1024]{2,1,0:T(8,128)} %bitcast.51), calls=%async_computation.2 | async-start | bytes 1048576 | tf_op jit(solution)/shard_map/all_to_all | solution.py:213
  29.7 58.4 %copy-start = (f32[2,1024]{1,0:T(2,128)S(1)}, f32[2,1024]{1,0:T(2,128)}, u32[]{:S(2)}) copy-start(f32[2,1024]{1,0:T(2,128)} %b_ref.3) | copy-start | bytes 24580
  29.8 17.0 %collective-permute-start = (f32[128,1024]{1,0:T(8,128)}, f32[128,1024]{1,0:T(8,128)S(1)}, u32[]{:S(2)}, u32[]{:S(2)}) collective-permute-start(f32[128,1024]{1,0:T(8,128)} %bitcast.52), channel_id=1, source_target_pairs={{0,32},{32,64},{64,96},{96,128},{128,160},{160,192},{192,224},{224... | collective-permute-start | bytes 1572872 | tf_op jit(solution)/shard_map/ppermute | solution.py:20
  40.8 13.9 %all-to-all-start.1 = ((f32[16,8,1024]{2,1,0:T(8,128)}), f32[16,8,1024]{2,1,0:T(8,128)S(1)}, u32[]{:S(2)}, u32[]{:S(2)}) async-start(f32[16,8,1024]{2,1,0:T(8,128)} %bitcast.53), calls=%async_computation.1 | async-start | bytes 1048576 | tf_op jit(solution)/shard_map/all_to_all | solution.py:212
  46.6 178.5 %reduce-scatter.2.cloned.1.call-start = ((), (), s32[]{:S(2)}) async-start(), calls=%async_computation.8 | async-start | bytes 2228224 | tf_op jit(solution)/shard_map/reduce_scatter | solution.py:256
  147.6 4.7 %collective-permute-start.2 = (bf16[4,128,1024]{2,1,0:T(8,128)(2,1)S(1)}, bf16[4,128,1024]{2,1,0:T(8,128)(2,1)}, u32[]{:S(2)}, u32[]{:S(2)}) collective-permute-start(bf16[4,128,1024]{2,1,0:T(8,128)(2,1)S(1)} %scaled.1.mine_ref), channel_id=1, source_target_pairs={{0,1},{1,0},{2,3},{3,2},{4,5},{5,4},{6,7},{7,6},{8,9},{9,8},{10,11... | collective-permute-start | bytes 3145736 | tf_op jit(solution)/shard_map/ppermute | solution.py:242
  159.0 1.7 copy-start.1
  159.0 1.7 copy-start.2
  159.0 1.7 copy-start.5
Sparse Core Ops, SparseCore 0:
  10.1 78.0 all-gather.2
  155.6 69.4 reduce-scatter.1

commit v5 on v4

--- a/solution.py
+++ b/solution.py
@@ -148,18 +148,30 @@
             adjoint = jnp.concatenate(parts, 1)
 
 
-def grads_kernel(core_ref, mine_ref, theirs_ref, both_ref, picked, sums, sems):
+def grads_kernel(
+    core_ref, mine_ref, theirs_hbm, both_ref, picked, sums, sems, theirs_ref, arrived
+):
     layers = sums.shape[1]
     chips, _, rows, width = sums.shape
     first = core_ref[0] == 0
     deep = mine_ref.shape[1]
     copies = []
+    coming = [
+        pltpu.make_async_copy(theirs_hbm.at[i], theirs_ref.at[i], arrived.at[i])
+        for i in range(2 * layers)
+    ]
+    for l in range(layers):
+        coming[l].start()
+        coming[layers + l].start()
     for l in range(layers):
         for at, ref in ((0, mine_ref), (deep, theirs_ref)):
+            if at:
+                coming[l].wait()
             turned = ref[l].T.reshape(chips, 2, rows, deep)
             picked[:, at : at + deep] = square(
                 jnp.where(first, turned[:, 0], turned[:, 1])
             )
+        coming[layers + l].wait()
         scaled = jnp.concatenate([mine_ref[layers + l], theirs_ref[layers + l]], 0)
         grad = step_size * jnp.dot(picked[...], scaled, preferred_element_type=f32)
         sums[:, l] = grad.reshape(chips, rows, width).astype(bf16)
@@ -242,17 +254,23 @@
     theirs = lax.ppermute(mine, "c", [(0, 1), (1, 0)])
     both = pl.pallas_call(
         grads_kernel,
-        in_specs=[pl.BlockSpec(memory_space=pltpu.SMEM), VMEM, VMEM],
+        in_specs=[
+            pl.BlockSpec(memory_space=pltpu.SMEM),
+            VMEM,
+            pl.BlockSpec(memory_space=pl.ANY),
+        ],
         out_specs=pl.BlockSpec(memory_space=pl.ANY),
         out_shape=FAR(part, bf16),
         scratch_shapes=[
             pltpu.VMEM((width // cores, cores * rows), bf16),
             pltpu.VMEM(part, bf16),
             pltpu.SemaphoreType.DMA((layers,)),
+            pltpu.VMEM(mine.shape, bf16),
+            pltpu.SemaphoreType.DMA((2 * layers,)),
         ],
         compiler_params=SMALL,
         name="grads",
-    )(core, near(mine), near(theirs))
+    )(core, near(mine), theirs)
     total = lax.psum_scatter(both, "z", scatter_dimension=0, tiled=True)
     adjoint = end_adj.astype(f32)
     for l in reversed(range(layers)):

time: 234 us -> 235 us (level)
  no operation moved by 1% of the time
where the time goes in v5:
time: 235 us; the launch traced here: 234 us
  waiting for transfers between devices  118 us (50%)
  blocking collectives  48.4 us (21%)
  starting transfers between devices  28.5 us (12%)
  Pallas kernels  14.2 us (6%)
  between operations  14.2 us (6%)
  local copies, waits for them, and re-layouts  4.82 us (2%)
  other arithmetic  2.98 us (1%)
  matrix products  2.5 us (1%)
    reduce_scatter x1, waiting for transfers between devices, local(): total = lax.psum_scatter(both, 'z', scatter_dimension=0, tiled=True)  63.2 us
    all_gather x1, waiting for transfers between devices, local(): full_weights = lax.all_gather(weights, ('z', 'c'))  33.4 us
    all_to_all x2, blocking collectives, corrected(): mine = lax.all_to_all(pieces, 'layer', 0, 0)  25.2 us
    all_to_all x2, blocking collectives, corrected(): return lax.all_to_all(starts, 'layer', 0, 0).reshape(rows, width)  23.2 us
    pallas_call x3, Pallas kernels, call(): pl.pallas_call(kernel, in_specs=[pl.BlockSpec(memory_space=pl.ANY)] + [VM...  10.8 us
    all_to_all x1, starting transfers between devices, local(): lax.all_to_all(jnp.broadcast_to(gains[None], (count, 1, width)), 'layer',...  9.13 us
    all_to_all x1, waiting for transfers between devices, local(): guess_rows = lax.all_to_all(guess.reshape(by_block), 'layer', 0, 0)  7.96 us
    all_to_all x1, waiting for transfers between devices, local(): lam_rows = lax.all_to_all(lam.reshape(by_block), 'layer', 0, 0)  6.93 us
  transfers between devices with their start and end apart: 8, of which 6 were waited for; matrix products, arithmetic and copies ran while one was open for 4% of the time, Pallas kernels for 0%

profile of v5, /device:TPU:6, one launch (start us, length us, event | category | flops | bytes accessed | tf_op | source)
XLA Modules:
  0.0 233.7 jit_solution(10203859935259365028)
XLA Ops:
  7.2 0.7 all-gather.3.cloned.1.call-update
  7.9 1.4 broadcast_in_dim.21
  9.3 9.1 %all-to-all-start = ((f32[16,1,1024]{2,1,0:T(1,128)}), f32[16,1,1024]{2,1,0:T(1,128)S(1)}, u32[]{:S(2)}, u32[]{:S(2)}) async-start(f32[16,1,1024]{2,1,0:T(1,128)} %broadcast_in_dim.21), calls=%async_computation | async-start | bytes 131072 | tf_op jit(solution)/shard_map/all_to_all | solution.py:220
  18.4 2.7 %collective-permute-start.1 = (f32[128,1024]{1,0:T(8,128)}, f32[128,1024]{1,0:T(8,128)S(1)}, u32[]{:S(2)}, u32[]{:S(2)}) collective-permute-start(f32[128,1024]{1,0:T(8,128)} %bitcast.50), channel_id=1, source_target_pairs={{32,0},{64,32},{96,64},{128,96},{160,128},{192,160},{224,192},{256... | collective-permute-start | bytes 1572872 | tf_op jit(solution)/shard_map/ppermute | solution.py:20
  21.2 3.1 %all-to-all-done = f32[16,1,1024]{2,1,0:T(1,128)S(1)} async-done(((f32[16,1,1024]{2,1,0:T(1,128)}), f32[16,1,1024]{2,1,0:T(1,128)S(1)}, u32[]{:S(2)}, u32[]{:S(2)}) %all-to-all-start) | async-done | bytes 65568 | tf_op jit(solution)/shard_map/all_to_all | solution.py:220
  24.2 5.5 %all-to-all-start.2 = ((f32[16,8,1024]{2,1,0:T(8,128)}), f32[16,8,1024]{2,1,0:T(8,128)S(1)}, u32[]{:S(2)}, u32[]{:S(2)}) async-start(f32[16,8,1024]{2,1,0:T(8,128)} %bitcast.51), calls=%async_computation.2 | async-start | bytes 1048576 | tf_op jit(solution)/shard_map/all_to_all | solution.py:225
  29.8 3.4 %collective-permute-start = (f32[128,1024]{1,0:T(8,128)}, f32[128,1024]{1,0:T(8,128)S(1)}, u32[]{:S(2)}, u32[]{:S(2)}) collective-permute-start(f32[128,1024]{1,0:T(8,128)} %bitcast.52), channel_id=1, source_target_pairs={{0,32},{32,64},{64,96},{96,128},{128,160},{160,192},{192,224},{224... | collective-permute-start | bytes 1572872 | tf_op jit(solution)/shard_map/ppermute | solution.py:20
  33.1 0.7 constant_dynamic-slice_fusion
  33.9 6.9 %all-to-all-done.2.guess_ref = f32[16,8,1024]{2,1,0:T(8,128)S(1)} async-done(((f32[16,8,1024]{2,1,0:T(8,128)}), f32[16,8,1024]{2,1,0:T(8,128)S(1)}, u32[]{:S(2)}, u32[]{:S(2)}) %all-to-all-start.2) | async-done | bytes 524320 | tf_op jit(solution)/shard_map/all_to_all | solution.py:225
  40.8 5.8 %all-to-all-start.1 = ((f32[16,8,1024]{2,1,0:T(8,128)}), f32[16,8,1024]{2,1,0:T(8,128)S(1)}, u32[]{:S(2)}, u32[]{:S(2)}) async-start(f32[16,8,1024]{2,1,0:T(8,128)} %bitcast.53), calls=%async_computation.1 | async-start | bytes 1048576 | tf_op jit(solution)/shard_map/all_to_all | solution.py:224
  46.7 0.1 convert_select_fusion.adj_ref
  46.8 0.1 convert_select_fusion.1.start_ref
  46.8 8.0 %all-to-all-done.1.guess_ref = f32[16,8,1024]{2,1,0:T(8,128)S(1)} async-done(((f32[16,8,1024]{2,1,0:T(8,128)}), f32[16,8,1024]{2,1,0:T(8,128)S(1)}, u32[]{:S(2)}, u32[]{:S(2)}) %all-to-all-start.1) | async-done | bytes 524320 | tf_op jit(solution)/shard_map/all_to_all | solution.py:224
  54.8 33.4 %all-gather.3.cloned.1.call-done = bf16[64,32,1024]{2,1,0:T(8,128)(2,1)} async-done(((bf16[2,32,1024]{2,1,0:T(8,128)(2,1)}), bf16[64,32,1024]{2,1,0:T(8,128)(2,1)}) %all-gather.3.cloned.1.call-update) | async-done | bytes 4194320 | tf_op jit(solution)/shard_map/all_gather | solution.py:210
  88.2 3.3 %relax.1 = (f32[128,1024]{1,0:T(8,128)}, bf16[128,1024]{1,0:T(8,128)(2,1)S(1)}) custom-call(bf16[32,2,32,1024]{3,2,1,0:T(8,128)(2,1)} %bitcast.44, f32[128,1024]{1,0:T(8,128)S(1)} %convert_select_fusion.1.start_ref, f32[2,1024]{1,0:T(2,128)S(1)} %copy-done), custom_call_target="tpu_custom_call" | custom-call | tf_op jit(solution)/shard_map/relax/pallas_call | solution.py:195
  91.5 13.7 %all_to_all.35.ends_ref = bf16[16,8,1024]{2,1,0:T(8,128)(2,1)S(1)} all-to-all(bf16[16,8,1024]{2,1,0:T(8,128)(2,1)S(1)} %bitcast.43), channel_id=1, replica_groups=mesh['layer'=16,'z'=16,'c'=2] {'layer'}, dimensions={0} | all-to-all | bytes 524288 | tf_op jit(solution)/shard_map/all_to_all | solution.py:40
  105.1 0.1 coarse_scan.2
  105.2 11.6 %all_to_all.36 = bf16[16,8,1024]{2,1,0:T(8,128)(2,1)S(1)} all-to-all(bf16[16,8,1024]{2,1,0:T(8,128)(2,1)S(1)} %coarse_scan.2), channel_id=1, replica_groups=mesh['layer'=16,'z'=16,'c'=2] {'layer'}, dimensions={0} | all-to-all | bytes 524288 | tf_op jit(solution)/shard_map/all_to_all | solution.py:49
  116.8 4.7 %both_ways.1 = (f32[128,1024]{1,0:T(8,128)}, bf16[1,128,1024]{2,1,0:T(8,128)(2,1)S(1)}, f32[2,128,1024]{2,1,0:T(8,128)S(1)}, f32[128,1024]{1,0:T(8,128)}, bf16[128,1024]{1,0:T(8,128)(2,1)S(1)}) custom-call(bf16[32,2,32,1024]{3,2,1,0:T(8,128)(2,1)} %bitcast.45, bf16[128,1024]{1,0:T(8,128)(2,1)S(1)} %bitcast.37, f32[2,1024]{1,0:T(2,128)S(1)} %copy-done, ...), custom_call_target="tpu_custom_call" | custom-call | tf_op jit(solution)/shard_map/both_ways/pallas_call | solution.py:195
  121.5 11.6 %all_to_all.37.ends_ref = bf16[16,8,1024]{2,1,0:T(8,128)(2,1)S(1)} all-to-all(bf16[16,8,1024]{2,1,0:T(8,128)(2,1)S(1)} %bitcast.42), channel_id=1, replica_groups=mesh['layer'=16,'z'=16,'c'=2] {'layer'}, dimensions={0} | all-to-all | bytes 524288 | tf_op jit(solution)/shard_map/all_to_all | solution.py:40
  133.1 0.1 coarse_scan.3
  133.2 11.6 %all_to_all.38 = bf16[16,8,1024]{2,1,0:T(8,128)(2,1)S(1)} all-to-all(bf16[16,8,1024]{2,1,0:T(8,128)(2,1)S(1)} %coarse_scan.3), channel_id=1, replica_groups=mesh['layer'=16,'z'=16,'c'=2] {'layer'}, dimensions={0} | all-to-all | bytes 524288 | tf_op jit(solution)/shard_map/all_to_all | solution.py:49
  144.8 2.8 %scaled.1.mine_ref = bf16[4,128,1024]{2,1,0:T(8,128)(2,1)S(1)} custom-call(bf16[32,2,32,1024]{3,2,1,0:T(8,128)(2,1)} %bitcast.46, bf16[128,1024]{1,0:T(8,128)(2,1)S(1)} %bitcast.39, f32[2,128,1024]{2,1,0:T(8,128)S(1)} %get-tuple-element.29.slopes_ref, bf16[128,1024]{1,0:T(8,128)(2,1)S(1)} %bitcast.38, bf16[1,128,1024]{2,1,0:T(8,128)(2,1)S(1)} %get-tuple-element.30.kept_ref), custom_call_target="tpu_custom_call" | custom-call | tf_op jit(solution)/shard_map/scaled/pallas_call | solution.py:195
  147.6 1.9 collective-permute-start.2
  149.6 2.8 %collective-permute-done.2.theirs_hbm = bf16[4,128,1024]{2,1,0:T(8,128)(2,1)} collective-permute-done((bf16[4,128,1024]{2,1,0:T(8,128)(2,1)S(1)}, bf16[4,128,1024]{2,1,0:T(8,128)(2,1)}, u32[]{:S(2)}, u32[]{:S(2)}) %collective-permute-start.2) | collective-permute-done | bytes 1048608 | tf_op jit(solution)/shard_map/ppermute | solution.py:254
  152.3 3.2 %grads.1 = bf16[16,2,32,1024]{3,2,1,0:T(8,128)(2,1)} custom-call(s32[1]{0:T(128)} %bitcast.16.core_ref, bf16[4,128,1024]{2,1,0:T(8,128)(2,1)S(1)} %scaled.1.mine_ref, bf16[4,128,1024]{2,1,0:T(8,128)(2,1)} %collective-permute-done.2.theirs_hbm), custom_call_target="tpu_custom_call" | custom-call | tf_op jit(solution)/shard_map/grads/pallas_call | solution.py:255
  155.5 2.7 %fusion.6 = (bf16[32,1,32,1024]{3,2,1,0:T(8,128)(2,1)S(1)}, bf16[32,1,32,1024]{3,2,1,0:T(8,128)(2,1)S(1)}) fusion(bf16[32,2,32,1024]{3,2,1,0:T(8,128)(2,1)} %bitcast.47), kind=kLoop, calls=%fused_computation.18 | loop fusion | bytes 8388608 | tf_op jit(solution)/shard_map/slice | solution.py:277
  158.2 0.9 fusion.2
  159.1 1.6 fusion.1
  160.8 1.2 fusion.5
  162.0 63.2 %reduce-scatter.2.cloned.1.call-done = bf16[1,2,32,1024]{3,2,1,0:T(8,128)(2,1)} async-done(((bf16[16,2,32,1024]{3,2,1,0:T(8,128)(2,1)}), bf16[1,2,32,1024]{3,2,1,0:T(8,128)(2,1)}) %reduce-scatter.2.cloned.1.call-update) | async-done | bytes 131088 | tf_op jit(solution)/shard_map/reduce_scatter | solution.py:274
  225.2 1.6 bitcast_convert_fusion
  (18 shorter events, 0.1 us)
Async XLA Ops:
  7.2 39.5 %copy-start.3 = (bf16[128,1024]{1,0:T(8,128)(2,1)S(1)}, bf16[128,1024]{1,0:T(8,128)(2,1)}, u32[]{:S(2)}) copy-start(bf16[128,1024]{1,0:T(8,128)(2,1)} %param.13) | copy-start | bytes 786436
  7.2 39.6 %copy-start.4 = (bf16[128,1024]{1,0:T(8,128)(2,1)S(1)}, bf16[128,1024]{1,0:T(8,128)(2,1)}, u32[]{:S(2)}) copy-start(bf16[128,1024]{1,0:T(8,128)(2,1)} %param.7) | copy-start | bytes 786436
  7.2 81.0 %all-gather.3.cloned.1.call-start = ((), (), s32[]{:S(2)}) async-start(), calls=%async_computation.9 | async-start | bytes 4325376 | tf_op jit(solution)/shard_map/all_gather | solution.py:210
  9.3 14.9 %all-to-all-start = ((f32[16,1,1024]{2,1,0:T(1,128)}), f32[16,1,1024]{2,1,0:T(1,128)S(1)}, u32[]{:S(2)}, u32[]{:S(2)}) async-start(f32[16,1,1024]{2,1,0:T(1,128)} %broadcast_in_dim.21), calls=%async_computation | async-start | bytes 131072 | tf_op jit(solution)/shard_map/all_to_all | solution.py:220
  18.4 28.2 %collective-permute-start.1 = (f32[128,1024]{1,0:T(8,128)}, f32[128,1024]{1,0:T(8,128)S(1)}, u32[]{:S(2)}, u32[]{:S(2)}) collective-permute-start(f32[128,1024]{1,0:T(8,128)} %bitcast.50), channel_id=1, source_target_pairs={{32,0},{64,32},{96,64},{128,96},{160,128},{192,160},{224,192},{256... | collective-permute-start | bytes 1572872 | tf_op jit(solution)/shard_map/ppermute | solution.py:20
  24.2 16.6 %all-to-all-start.2 = ((f32[16,8,1024]{2,1,0:T(8,128)}), f32[16,8,1024]{2,1,0:T(8,128)S(1)}, u32[]{:S(2)}, u32[]{:S(2)}) async-start(f32[16,8,1024]{2,1,0:T(8,128)} %bitcast.51), calls=%async_computation.2 | async-start | bytes 1048576 | tf_op jit(solution)/shard_map/all_to_all | solution.py:225
  29.7 58.4 %copy-start = (f32[2,1024]{1,0:T(2,128)S(1)}, f32[2,1024]{1,0:T(2,128)}, u32[]{:S(2)}) copy-start(f32[2,1024]{1,0:T(2,128)} %b_ref.3) | copy-start | bytes 24580
  29.8 17.0 %collective-permute-start = (f32[128,1024]{1,0:T(8,128)}, f32[128,1024]{1,0:T(8,128)S(1)}, u32[]{:S(2)}, u32[]{:S(2)}) collective-permute-start(f32[128,1024]{1,0:T(8,128)} %bitcast.52), channel_id=1, source_target_pairs={{0,32},{32,64},{64,96},{96,128},{128,160},{160,192},{192,224},{224... | collective-permute-start | bytes 1572872 | tf_op jit(solution)/shard_map/ppermute | solution.py:20
  40.8 13.9 %all-to-all-start.1 = ((f32[16,8,1024]{2,1,0:T(8,128)}), f32[16,8,1024]{2,1,0:T(8,128)S(1)}, u32[]{:S(2)}, u32[]{:S(2)}) async-start(f32[16,8,1024]{2,1,0:T(8,128)} %bitcast.53), calls=%async_computation.1 | async-start | bytes 1048576 | tf_op jit(solution)/shard_map/all_to_all | solution.py:224
  46.6 178.6 %reduce-scatter.2.cloned.1.call-start = ((), (), s32[]{:S(2)}) async-start(), calls=%async_computation.8 | async-start | bytes 2228224 | tf_op jit(solution)/shard_map/reduce_scatter | solution.py:274
  147.6 4.7 %collective-permute-start.2 = (bf16[4,128,1024]{2,1,0:T(8,128)(2,1)S(1)}, bf16[4,128,1024]{2,1,0:T(8,128)(2,1)}, u32[]{:S(2)}, u32[]{:S(2)}) collective-permute-start(bf16[4,128,1024]{2,1,0:T(8,128)(2,1)S(1)} %scaled.1.mine_ref), channel_id=1, source_target_pairs={{0,1},{1,0},{2,3},{3,2},{4,5},{5,4},{6,7},{7,6},{8,9},{9,8},{10,11... | collective-permute-start | bytes 3145736 | tf_op jit(solution)/shard_map/ppermute | solution.py:254
  159.1 1.7 copy-start.1
  159.1 1.7 copy-start.2
  159.1 1.7 copy-start.5
Sparse Core Ops, SparseCore 0:
  10.1 78.0 all-gather.2
  155.7 69.5 reduce-scatter.1
